TPU v7x, 32 devices: a whole 2x2x4 slice. The times are simulated.
32 devices in a mesh: doc: 8 (over y, x, core), vocab: 4 (over z).
Axes of the slice: x: 2, y: 2, z: 4, core: 2. Of those that a mesh axis runs over, the one named last changes fastest.
Arguments:
- tile_values: bfloat16 [8, 4, 24, 128, 128], P('doc', 'vocab'), may hold values from -6 to 6
- tile_rows: int32 [8, 4, 24], P('doc', 'vocab'), may hold values from 0 to 7, as said below
- tile_columns: int32 [8, 4, 24], P('doc', 'vocab'), may hold values from 0 to 3
- counts: int32 [8, 4], P('doc', 'vocab'), may hold values from 7 to 24, as said below
- sketch: bfloat16 [2048, 512], P('vocab'), may hold values from -6 to 6
- query_tiles: int32 [2048, 4, 4], P('doc', 'vocab'), may hold values from 0 to 3
- query_values: float32 [2048, 4, 4, 128], P('doc', 'vocab'), may hold values from -6 to 6
Outputs:
- term_basis: float32 [4, 512, 512], P('vocab', 'doc')
- projections: float32 [2048, 512], P('doc')
Inputs may be any that keep to these rules, and one draw needn't show every extreme that they name: Each device uses its first counts slots; some device uses all 24 slots in every draw. The (tile_rows, tile_columns) pairs of one device's 24 slots are all different. `query_tiles`: A query may name the same term block more than once; the values then add.
All inputs are finite; a program needn't handle non-finite values.
Results may differ from a plain program's by a relative error of at most 0.0016.
Values may be sent and summed in bfloat16 or wider, within the bound.
No kernel may reach another device: no remote copies, remote signals or barrier semaphores. Data moves between devices by JAX's collectives and lax.ppermute only.
A program may use at most 64 MiB of HBM per device.

v0:
```python
import jax
import jax.numpy as jnp
from jax import lax
from jax.experimental import pallas as pl
from jax.experimental.pallas import tpu as pltpu
from jax.sharding import PartitionSpec as P


ROW_TILES = 8
PANEL = 32
TILE = 128
CORES = 2
HALVES = 2

precise = lax.Precision.HIGHEST
smem = pl.BlockSpec(memory_space=pltpu.SMEM)
vmem = pl.BlockSpec(memory_space=pltpu.VMEM)
f32 = jnp.float32
bf16 = jnp.bfloat16


def dot(left, right, dims, precision=None):
    return lax.dot_general(
        left, right, (dims, ((), ())), precision=precision, preferred_element_type=f32
    )


def invert_factor(work):
    tiles = work.shape[0] // TILE
    chunks = PANEL // 8
    panels = TILE // PANEL
    sub_id = lax.broadcasted_iota(jnp.int32, (8, TILE), 0)
    lane_id = lax.broadcasted_iota(jnp.int32, (8, TILE), 1)

    def block(o, carry):
        base = pl.multiple_of(o * TILE, TILE)
        for s in range(panels):
            lo = s * PANEL
            at = base + lo
            own = [work[pl.ds(at + 8 * r, 8), pl.ds(base, TILE)] for r in range(chunks)]
            col = [[None] * chunks for _ in range(PANEL)]
            for l in range(PANEL):
                for r in range(l // 8, chunks):
                    col[l][r] = jnp.broadcast_to(own[r][:, lo + l : lo + l + 1], (8, TILE))
            in_panel = (lane_id >= lo) & (lane_id < lo + PANEL)
            rows = []
            for r in range(chunks):
                eye = (lane_id == lo + 8 * r + sub_id).astype(f32)
                line = []
                for t in range(tiles):
                    old = work[pl.ds(at + 8 * r, 8), t * TILE : (t + 1) * TILE]
                    line.append(jnp.where(in_panel & (o == t), eye, old))
                rows.append(line)
            for k in range(PANEL):
                kr, ks = k // 8, k % 8
                pivot = jnp.broadcast_to(col[k][kr][ks : ks + 1, :], (8, TILE))
                q = lax.rsqrt(pivot)
                lcol = [None] * chunks
                for r in range(kr, chunks):
                    lcol[r] = col[k][r] * q
                for l in range(k + 1, PANEL):
                    e = jnp.broadcast_to(lcol[l // 8][l % 8 : l % 8 + 1, :], (8, TILE))
                    for r in range(l // 8, chunks):
                        col[l][r] = col[l][r] - lcol[r] * e
                below = jnp.where(sub_id > ks, lcol[kr], 0.0)
                for t in range(tiles):
                    rk = jnp.broadcast_to(rows[kr][t][ks : ks + 1, :], (8, TILE)) * q
                    rows[kr][t] = jnp.where(sub_id == ks, rk, rows[kr][t] - below * rk)
                    for r in range(kr + 1, chunks):
                        rows[r][t] = rows[r][t] - lcol[r] * rk
            for r in range(chunks):
                for t in range(tiles):
                    work[pl.ds(at + 8 * r, 8), t * TILE : (t + 1) * TILE] = rows[r][t]
            if s + 1 < panels:
                left = work[pl.ds(at, PANEL), pl.ds(base, TILE)]
                full = work[pl.ds(at, PANEL), :]
                update = dot(left, full, ((0,), (0,)), precise)
                first = lo + PANEL
                count = TILE - first
                lanes = lax.broadcasted_iota(jnp.int32, (count, TILE), 1)
                gone = (lanes >= lo) & (lanes < lo + PANEL)
                for t in range(tiles):
                    span = slice(t * TILE, (t + 1) * TILE)
                    old = work[pl.ds(base + first, count), span]
                    old = jnp.where(gone & (o == t), 0.0, old)
                    work[pl.ds(base + first, count), span] = old - update[first:, span]
        square = work[pl.ds(base, TILE), pl.ds(base, TILE)]
        lower = lax.broadcasted_iota(jnp.int32, (TILE, TILE), 0) >= lax.broadcasted_iota(
            jnp.int32, (TILE, TILE), 1
        )
        work[pl.ds(base, TILE), pl.ds(base, TILE)] = jnp.where(lower, square, 0.0)

        def later(b, inner):
            below_at = pl.multiple_of(b * TILE, TILE)
            left = work[pl.ds(base, TILE), pl.ds(below_at, TILE)]
            update = dot(left, work[pl.ds(base, TILE), :], ((0,), (0,)), precise)
            work[pl.ds(below_at, TILE), pl.ds(base, TILE)] = jnp.zeros((TILE, TILE), f32)
            work[pl.ds(below_at, TILE), :] = work[pl.ds(below_at, TILE), :] - update
            return inner

        lax.fori_loop(o + 1, tiles, later, 0)
        return carry

    lax.fori_loop(0, tiles, block, 0)


def dense_kernel(where, halves, places, at_rows, at_columns, used, tiles, *refs):
    outs, dense = refs[:-1], refs[-1]
    rows = dense.shape[0] // len(outs)
    dense[...] = jnp.zeros_like(dense)

    def place(s, carry):
        r = pl.multiple_of(at_rows[0, s] * TILE, TILE)
        c = pl.multiple_of(at_columns[0, s] * TILE, TILE)
        dense[pl.ds(r, TILE), pl.ds(c, TILE)] = tiles[s]
        return carry

    lax.fori_loop(0, used[0, 0], place, 0)
    for i, out in enumerate(outs):
        block = lax.bitwise_xor(where[0], places[i // halves]) * halves + i % halves
        out[...] = dense[pl.ds(pl.multiple_of(block * rows, rows), rows), :]


def turn_kernel(*refs):
    blocks, out = refs[:-1], refs[-1]
    whole = jnp.concatenate([block[...] for block in blocks], axis=0)
    out[...] = whole.T


def assemble_kernel(where, places, *refs):
    pieces, out = refs[:-1], refs[-1]
    rows = pieces[0].shape[1]
    for piece, place in zip(pieces, places):
        at = pl.multiple_of(lax.bitwise_xor(where[1], place) * rows, rows)
        out[:, pl.ds(at, rows), :] = piece[...]


def forward_kernel(*refs):
    blocks = refs[:-3]
    own_sketch, others, out = refs[-3:]
    total = dot(blocks[0][...], own_sketch[...], ((1,), (0,)))
    for s in range(1, len(blocks)):
        total = total + dot(blocks[s][...], others[s - 1], ((1,), (0,)))
    out[...] = total.astype(bf16)


def backward_kernel(where, places, turned, *refs):
    outs = refs[-2 - len(places) : -2]
    sketched = refs[: -2 - len(places)]
    whole, full = refs[-2:]
    height = sketched[0].shape[0]
    for i, piece in enumerate(sketched):
        whole[i * height : (i + 1) * height, :] = piece[...]
    full[...] = dot(turned[...], whole[...], ((1,), (0,)))
    rows = outs[0].shape[0]
    for out, place in zip(outs, places):
        at = pl.multiple_of(lax.bitwise_xor(where[1], place) * rows, rows)
        out[...] = full[pl.ds(at, rows), :]


def gram_kernel(where, places, *refs):
    pieces = refs[: len(places)]
    gram, back, product = refs[len(places) :]
    rows = pieces[0].shape[0]
    for i, piece in enumerate(pieces):
        back[i * rows : (i + 1) * rows, :] = piece[...]
    share = gram.shape[0]
    start = where[1] * share
    tile_at = pl.multiple_of(start // TILE * TILE, TILE)
    product[...] = dot(back[:, pl.ds(tile_at, TILE)], back[...], ((0,), (0,)), precise)
    gram[...] = product[pl.ds(pl.multiple_of(start - tile_at, share), share), :]


def query_dense_kernel(tiles, values, out):
    for c in range(out.shape[1] // TILE):
        total = None
        for j in range(tiles.shape[1]):
            part = jnp.where(tiles[:, j : j + 1] == c, values[:, j * TILE : (j + 1) * TILE], 0.0)
            total = part if total is None else total + part
        out[:, c * TILE : (c + 1) * TILE] = total


def query_kernel(where, places, v_places, dense, *refs):
    pieces = refs[: len(places)]
    outs = refs[len(places) : -2]
    back, full = refs[-2:]
    height = pieces[0].shape[0]
    for piece, place in zip(pieces, places):
        at = pl.multiple_of(lax.bitwise_xor(where[1], place) * height, height)
        back[pl.ds(at, height), :] = piece[...]
    full[...] = dot(dense[...], back[...], ((1,), (0,)), precise)
    rows = outs[0].shape[0]
    for out, place in zip(outs, v_places):
        at = pl.multiple_of(lax.bitwise_xor(where[0], place) * rows, rows)
        out[...] = full[pl.ds(at, rows), :]


def factor_kernel(where, places, scale, *refs):
    pieces, out, work = refs[: len(places)], refs[-2], refs[-1]
    rows = pieces[0].shape[0]
    for piece, place in zip(pieces, places):
        at = pl.multiple_of(lax.bitwise_xor(where[1], place) * rows, rows)
        work[pl.ds(at, rows), :] = piece[...] * scale
    invert_factor(work)
    n = work.shape[0]
    lower = lax.broadcasted_iota(jnp.int32, (n, n), 0) >= lax.broadcasted_iota(jnp.int32, (n, n), 1)
    out[...] = jnp.where(lower, work[...], 0.0)


def output_kernel(where, v_places, *refs):
    inverse, own = refs[0], refs[1]
    coords = refs[2 : 2 + len(v_places)]
    basis, projections, full = refs[2 + len(v_places) :]
    rows = coords[0].shape[0]
    for piece, place in zip(coords, v_places):
        at = pl.multiple_of(lax.bitwise_xor(where[0], place) * rows, rows)
        full[pl.ds(at, rows), :] = piece[...]
    basis[...] = dot(own[...], inverse[...], ((1,), (1,)), precise)
    raw = dot(full[...], inverse[...], ((1,), (1,)), precise)
    mean = jnp.sum(raw * raw, axis=1, keepdims=True) * (1.0 / raw.shape[1])
    projections[...] = raw * lax.rsqrt(mean + 1e-06)


def call(kernel, outs, scratch, scalars, arrays, keep=True):
    if keep:
        outs = jax.tree.map(lambda x: pltpu.VMEM(x.shape, x.dtype), outs)
    return pl.pallas_call(
        kernel,
        out_shape=outs,
        in_specs=[smem] * len(scalars) + [vmem] * len(arrays),
        out_specs=jax.tree.map(lambda _: vmem, outs),
        scratch_shapes=scratch,
        compiler_params=pltpu.CompilerParams(vmem_limit_bytes=16 << 20),
    )(*scalars, *[pltpu.with_memory_space_constraint(x, pltpu.VMEM) for x in arrays])


def work(tile_values, tile_rows, tile_columns, counts, sketch, query_tiles, query_values):
    n_doc, n_vocab = lax.axis_size("doc"), lax.axis_size("vocab")
    doc, vocab = lax.axis_index("doc"), lax.axis_index("vocab")
    where = jnp.stack([vocab, doc]).astype(jnp.int32)
    chips = n_doc // CORES
    edge = tile_values.shape[3]
    terms, width = sketch.shape
    queries = query_tiles.shape[0]
    documents = ROW_TILES * edge
    share = terms // n_doc
    places = [CORES * m + c for m in range(chips) for c in range(CORES)]
    bits = [1 << b for b in reversed(range(n_vocab.bit_length() - 1))]
    v_places = [0]
    for bit in bits:
        v_places += [place | bit for place in v_places]

    def along(x, place):
        return lax.ppermute(x, "vocab", [(a, a ^ place) for a in range(n_vocab)])

    def across(x, place):
        return lax.ppermute(x, "doc", [(a, a ^ place) for a in range(n_doc)])

    def collect(x):
        held = [x]
        for bit in bits:
            near = along(x, bit)
            held += [near] + [along(piece, bit) for piece in held[1:]]
        return held

    def spread(x):
        near = [x]
        for m in range(1, chips):
            near.append(across(x, CORES * m))
        far = [across(piece, 1) for piece in near]
        return [piece for pair in zip(near, far) for piece in pair]

    rows = documents // n_vocab // HALVES
    dense = call(
        lambda where, *refs: dense_kernel(where, HALVES, v_places, *refs),
        [jax.ShapeDtypeStruct((rows, terms), bf16)] * (n_vocab * HALVES),
        [pltpu.VMEM((documents, terms), bf16)],
        [where, tile_rows[0], tile_columns[0], counts],
        [tile_values[0, 0]],
    )
    own_terms = lax.dynamic_slice_in_dim(sketch, doc * share, share, 0)
    blocks = [
        [dense[h]] + [along(dense[i * HALVES + h], v_places[i]) for i in range(1, n_vocab)]
        for h in range(HALVES)
    ]
    others = jnp.stack([along(own_terms, place) for place in v_places[1:]])
    term_pieces = spread(others)
    other_sketch = call(
        lambda where, *refs: assemble_kernel(where, places, *refs),
        jax.ShapeDtypeStruct((n_vocab - 1, terms, width), bf16),
        [],
        [where],
        term_pieces,
    )
    turned = call(turn_kernel, jax.ShapeDtypeStruct((terms, documents), bf16), [], [], dense)
    query_dense = call(
        query_dense_kernel,
        jax.ShapeDtypeStruct((queries, terms), f32),
        [],
        [],
        [query_tiles[:, 0], query_values.reshape(queries, -1)],
    )
    gathered = []
    for h in range(HALVES):
        own_sketched = call(
            forward_kernel,
            jax.ShapeDtypeStruct((rows, width), bf16),
            [],
            [],
            [*blocks[h], sketch, other_sketch],
        )
        gathered.append(collect(own_sketched))
    sketched = [gathered[h][i] for i in range(n_vocab) for h in range(HALVES)]
    piece = jax.ShapeDtypeStruct((share, width), f32)
    parted = call(
        lambda where, *refs: backward_kernel(where, places, *refs),
        [piece] * n_doc,
        [pltpu.VMEM((documents, width), bf16), pltpu.VMEM((terms, width), f32)],
        [where],
        [turned, *sketched],
    )
    paired = [parted[CORES * m] + across(parted[CORES * m + 1], 1) for m in range(chips)]
    own_back = paired[0]
    for m in range(1, chips):
        own_back = own_back + across(paired[m], CORES * m)
    back_pieces = spread(own_back)
    gram_share = width // n_doc
    gram_rows = call(
        lambda where, *refs: gram_kernel(where, places, *refs),
        jax.ShapeDtypeStruct((gram_share, width), f32),
        [pltpu.VMEM((terms, width), f32), pltpu.VMEM((TILE, width), f32)],
        [where],
        back_pieces,
    )
    for bit in reversed(bits):
        gram_rows = gram_rows + along(gram_rows, bit)
    query_rows = queries // n_vocab
    query_parts = call(
        lambda where, *refs: query_kernel(where, places, v_places, *refs),
        [jax.ShapeDtypeStruct((query_rows, width), f32)] * n_vocab,
        [pltpu.VMEM((terms, width), f32), pltpu.VMEM((queries, width), f32)],
        [where],
        [query_dense, *back_pieces],
    )
    gram_pieces = spread(gram_rows)
    own_query = query_parts[0]
    for i in range(1, n_vocab):
        own_query = own_query + along(query_parts[i], v_places[i])
    coords = [own_query] + [along(own_query, place) for place in v_places[1:]]
    inverse = call(
        lambda where, *refs: factor_kernel(where, places, 1.0 / (terms * n_vocab), *refs),
        jax.ShapeDtypeStruct((width, width), f32),
        [pltpu.VMEM((width, width), f32)],
        [where],
        gram_pieces,
    )
    basis, projections = call(
        lambda where, *refs: output_kernel(where, v_places, *refs),
        [
            jax.ShapeDtypeStruct((share, width), f32),
            jax.ShapeDtypeStruct((queries, width), f32),
        ],
        [pltpu.VMEM((queries, width), f32)],
        [where],
        [inverse, own_back, *coords],
        keep=False,
    )
    return basis[None], projections


def solution(mesh):
    return jax.shard_map(
        work,
        mesh=mesh,
        in_specs=(
            P("doc", "vocab", None, None, None),
            P("doc", "vocab", None),
            P("doc", "vocab", None),
            P("doc", "vocab"),
            P("vocab", None),
            P("doc", "vocab", None),
            P("doc", "vocab", None, None),
        ),
        out_specs=(P("vocab", "doc", None), P("doc", None)),
        check_vma=False,
    )
```

profile of v0, /device:TPU:0, one launch (start us, length us, event | category | flops | bytes accessed | tf_op | source)
XLA Modules:
  0.0 152.5 jit_solution(15430926055251140842)
XLA Ops:
  1.5 4.1 %collective-permute-start.3 = (bf16[64,512]{1,0:T(8,128)(2,1)S(1)}, bf16[64,512]{1,0:T(8,128)(2,1)S(1)}, u32[]{:S(2)}, u32[]{:S(2)}) collective-permute-start(bf16[64,512]{1,0:T(8,128)(2,1)S(1)} %constant_dynamic-slice_fusion), channel_id=1, source_target_pairs={{0,2},{1,3},{2,0},{3,1},{4,6},{5,7},{6,4},{7,5},{8,10},{9,11},{10,... | collective-permute-start | bytes 196616 | tf_op jit(solution)/shard_map/ppermute | solution.py:254
  5.5 1.6 %collective-permute-start.4 = (bf16[64,512]{1,0:T(8,128)(2,1)S(1)}, bf16[64,512]{1,0:T(8,128)(2,1)S(1)}, u32[]{:S(2)}, u32[]{:S(2)}) collective-permute-start(bf16[64,512]{1,0:T(8,128)(2,1)S(1)} %constant_dynamic-slice_fusion), channel_id=1, source_target_pairs={{0,1},{1,0},{2,3},{3,2},{4,5},{5,4},{6,7},{7,6},{8,9},{9,8},{10,11... | collective-permute-start | bytes 196616 | tf_op jit(solution)/shard_map/ppermute | solution.py:254
  9.8 3.4 %collective-permute-done.5 = bf16[64,512]{1,0:T(8,128)(2,1)S(1)} collective-permute-done((bf16[64,512]{1,0:T(8,128)(2,1)S(1)}, bf16[64,512]{1,0:T(8,128)(2,1)S(1)}, u32[]{:S(2)}, u32[]{:S(2)}) %collective-permute-start.5) | collective-permute-done | bytes 65568 | tf_op jit(solution)/shard_map/ppermute | solution.py:254
  13.2 1.6 %collective-permute-start.9 = (bf16[3,64,512]{2,1,0:T(8,128)(2,1)S(1)}, bf16[3,64,512]{2,1,0:T(8,128)(2,1)S(1)}, u32[]{:S(2)}, u32[]{:S(2)}) collective-permute-start(bf16[3,64,512]{2,1,0:T(8,128)(2,1)S(1)} %pad_maximum_fusion.refs_0_), channel_id=1, source_target_pairs={{0,16},{4,20},{8,24},{12,28},{16,0},{20,4},{24,8},{28,12},{1,17},{... | collective-permute-start | bytes 589832 | tf_op jit(solution)/shard_map/ppermute | solution.py:257
  17.5 4.1 %collective-permute-done.9.refs_4_ = bf16[3,64,512]{2,1,0:T(8,128)(2,1)S(1)} collective-permute-done((bf16[3,64,512]{2,1,0:T(8,128)(2,1)S(1)}, bf16[3,64,512]{2,1,0:T(8,128)(2,1)S(1)}, u32[]{:S(2)}, u32[]{:S(2)}) %collective-permute-start.9) | collective-permute-done | bytes 196640 | tf_op jit(solution)/shard_map/ppermute | solution.py:257
  27.2 2.6 %collective-permute-start.13 = (bf16[128,512]{1,0:T(8,128)(2,1)S(1)}, bf16[128,512]{1,0:T(8,128)(2,1)S(1)}, u32[]{:S(2)}, u32[]{:S(2)}) collective-permute-start(bf16[128,512]{1,0:T(8,128)(2,1)S(1)} %get-tuple-element.27.refs_3_), channel_id=1, source_target_pairs={{0,2},{1,3},{2,0},{3,1},{4,6},{5,7},{6,4},{7,5},{8,10},{9,11},{10,... | collective-permute-start | bytes 393224 | tf_op jit(solution)/shard_map/ppermute | solution.py:254
  29.9 7.0 %collective-permute-done.13.refs_1_ = bf16[128,512]{1,0:T(8,128)(2,1)S(1)} collective-permute-done((bf16[128,512]{1,0:T(8,128)(2,1)S(1)}, bf16[128,512]{1,0:T(8,128)(2,1)S(1)}, u32[]{:S(2)}, u32[]{:S(2)}) %collective-permute-start.13) | collective-permute-done | bytes 131104 | tf_op jit(solution)/shard_map/ppermute | solution.py:254
  36.9 1.8 %collective-permute-start.15 = (bf16[128,512]{1,0:T(8,128)(2,1)S(1)}, bf16[128,512]{1,0:T(8,128)(2,1)S(1)}, u32[]{:S(2)}, u32[]{:S(2)}) collective-permute-start(bf16[128,512]{1,0:T(8,128)(2,1)S(1)} %get-tuple-element.31.refs_7_), channel_id=1, source_target_pairs={{0,3},{1,2},{2,1},{3,0},{4,7},{5,6},{6,5},{7,4},{8,11},{9,10},{10,... | collective-permute-start | bytes 393224 | tf_op jit(solution)/shard_map/ppermute | solution.py:254
  38.7 1.7 %collective-permute-start = (bf16[128,512]{1,0:T(8,128)(2,1)S(1)}, bf16[128,512]{1,0:T(8,128)(2,1)S(1)}, u32[]{:S(2)}, u32[]{:S(2)}) collective-permute-start(bf16[128,512]{1,0:T(8,128)(2,1)S(1)} %get-tuple-element.26.refs_2_), channel_id=1, source_target_pairs={{0,2},{1,3},{2,0},{3,1},{4,6},{5,7},{6,4},{7,5},{8,10},{9,11},{10,... | collective-permute-start | bytes 393224 | tf_op jit(solution)/shard_map/ppermute | solution.py:254
  41.3 1.8 %collective-permute-start.2 = (bf16[128,512]{1,0:T(8,128)(2,1)S(1)}, bf16[128,512]{1,0:T(8,128)(2,1)S(1)}, u32[]{:S(2)}, u32[]{:S(2)}) collective-permute-start(bf16[128,512]{1,0:T(8,128)(2,1)S(1)} %get-tuple-element.30.refs_6_), channel_id=1, source_target_pairs={{0,3},{1,2},{2,1},{3,0},{4,7},{5,6},{6,5},{7,4},{8,11},{9,10},{10,... | collective-permute-start | bytes 393224 | tf_op jit(solution)/shard_map/ppermute | solution.py:254
  43.8 2.0 %collective-permute-done.14.refs_2_ = bf16[128,512]{1,0:T(8,128)(2,1)S(1)} collective-permute-done((bf16[128,512]{1,0:T(8,128)(2,1)S(1)}, bf16[128,512]{1,0:T(8,128)(2,1)S(1)}, u32[]{:S(2)}, u32[]{:S(2)}) %collective-permute-start.14) | collective-permute-done | bytes 131104 | tf_op jit(solution)/shard_map/ppermute | solution.py:254
  46.2 5.3 %collective-permute-start.17 = (bf16[128,512]{1,0:T(8,128)(2,1)S(1)}, bf16[128,512]{1,0:T(8,128)(2,1)S(1)}, u32[]{:S(2)}, u32[]{:S(2)}) collective-permute-start(bf16[128,512]{1,0:T(8,128)(2,1)S(1)} %shard_map.90.refs_2_), channel_id=1, source_target_pairs={{0,2},{1,3},{2,0},{3,1},{4,6},{5,7},{6,4},{7,5},{8,10},{9,11},{10,... | collective-permute-start | bytes 393224 | tf_op jit(solution)/shard_map/ppermute | solution.py:254
  51.5 7.0 %collective-permute-done.refs_1_ = bf16[128,512]{1,0:T(8,128)(2,1)S(1)} collective-permute-done((bf16[128,512]{1,0:T(8,128)(2,1)S(1)}, bf16[128,512]{1,0:T(8,128)(2,1)S(1)}, u32[]{:S(2)}, u32[]{:S(2)}) %collective-permute-start) | collective-permute-done | bytes 131104 | tf_op jit(solution)/shard_map/ppermute | solution.py:254
  59.0 3.8 %collective-permute-start.16 = (bf16[128,512]{1,0:T(8,128)(2,1)S(1)}, bf16[128,512]{1,0:T(8,128)(2,1)S(1)}, u32[]{:S(2)}, u32[]{:S(2)}) collective-permute-start(bf16[128,512]{1,0:T(8,128)(2,1)S(1)} %shard_map.89.refs_1_), channel_id=1, source_target_pairs={{0,2},{1,3},{2,0},{3,1},{4,6},{5,7},{6,4},{7,5},{8,10},{9,11},{10,... | collective-permute-start | bytes 393224 | tf_op jit(solution)/shard_map/ppermute | solution.py:254
  62.7 2.0 %collective-permute-start.18 = (bf16[128,512]{1,0:T(8,128)(2,1)S(1)}, bf16[128,512]{1,0:T(8,128)(2,1)S(1)}, u32[]{:S(2)}, u32[]{:S(2)}) collective-permute-start(bf16[128,512]{1,0:T(8,128)(2,1)S(1)} %shard_map.89.refs_1_), channel_id=1, source_target_pairs={{0,1},{1,0},{2,3},{3,2},{4,5},{5,4},{6,7},{7,6},{8,9},{9,8},{10,11... | collective-permute-start | bytes 393224 | tf_op jit(solution)/shard_map/ppermute | solution.py:254
  65.7 3.1 %collective-permute-done.16.refs_3_ = bf16[128,512]{1,0:T(8,128)(2,1)S(1)} collective-permute-done((bf16[128,512]{1,0:T(8,128)(2,1)S(1)}, bf16[128,512]{1,0:T(8,128)(2,1)S(1)}, u32[]{:S(2)}, u32[]{:S(2)}) %collective-permute-start.16) | collective-permute-done | bytes 131104 | tf_op jit(solution)/shard_map/ppermute | solution.py:254
  70.4 2.8 %collective-permute-done.18.refs_5_ = bf16[128,512]{1,0:T(8,128)(2,1)S(1)} collective-permute-done((bf16[128,512]{1,0:T(8,128)(2,1)S(1)}, bf16[128,512]{1,0:T(8,128)(2,1)S(1)}, u32[]{:S(2)}, u32[]{:S(2)}) %collective-permute-start.18) | collective-permute-done | bytes 131104 | tf_op jit(solution)/shard_map/ppermute | solution.py:254
  73.2 2.7 %collective-permute-done.21.refs_8_ = bf16[128,512]{1,0:T(8,128)(2,1)S(1)} collective-permute-done((bf16[128,512]{1,0:T(8,128)(2,1)S(1)}, bf16[128,512]{1,0:T(8,128)(2,1)S(1)}, u32[]{:S(2)}, u32[]{:S(2)}) %collective-permute-start.21) | collective-permute-done | bytes 131104 | tf_op jit(solution)/shard_map/ppermute | solution.py:254
  81.3 1.6 %collective-permute-start.26 = (f32[64,512]{1,0:T(8,128)S(1)}, f32[64,512]{1,0:T(8,128)S(1)}, u32[]{:S(2)}, u32[]{:S(2)}) collective-permute-start(f32[64,512]{1,0:T(8,128)S(1)} %add.43), channel_id=1, source_target_pairs={{0,16},{4,20},{8,24},{12,28},{16,0},{20,4},{24,8},{28,12},{1,17},{... | collective-permute-start | bytes 393224 | tf_op jit(solution)/shard_map/ppermute | solution.py:257
  83.8 2.4 %collective-permute-done.24 = f32[64,512]{1,0:T(8,128)S(1)} collective-permute-done((f32[64,512]{1,0:T(8,128)S(1)}, f32[64,512]{1,0:T(8,128)S(1)}, u32[]{:S(2)}, u32[]{:S(2)}) %collective-permute-start.24) | collective-permute-done | bytes 131104 | tf_op jit(solution)/shard_map/ppermute | solution.py:257
  86.2 3.3 %collective-permute-done.26 = f32[64,512]{1,0:T(8,128)S(1)} collective-permute-done((f32[64,512]{1,0:T(8,128)S(1)}, f32[64,512]{1,0:T(8,128)S(1)}, u32[]{:S(2)}, u32[]{:S(2)}) %collective-permute-start.26) | collective-permute-done | bytes 131104 | tf_op jit(solution)/shard_map/ppermute | solution.py:257
  93.1 2.5 %collective-permute-done.30.refs_2_.refs_3_ = f32[64,512]{1,0:T(8,128)S(1)} collective-permute-done((f32[64,512]{1,0:T(8,128)S(1)}, f32[64,512]{1,0:T(8,128)S(1)}, u32[]{:S(2)}, u32[]{:S(2)}) %collective-permute-start.30) | collective-permute-done | bytes 131104 | tf_op jit(solution)/shard_map/ppermute | solution.py:257
  95.6 2.4 %collective-permute-done.32.refs_4_.refs_5_ = f32[64,512]{1,0:T(8,128)S(1)} collective-permute-done((f32[64,512]{1,0:T(8,128)S(1)}, f32[64,512]{1,0:T(8,128)S(1)}, u32[]{:S(2)}, u32[]{:S(2)}) %collective-permute-start.32) | collective-permute-done | bytes 131104 | tf_op jit(solution)/shard_map/ppermute | solution.py:257
  100.9 5.7 %collective-permute-done.36 = f32[64,512]{1,0:T(8,128)S(1)} collective-permute-done((f32[64,512]{1,0:T(8,128)S(1)}, f32[64,512]{1,0:T(8,128)S(1)}, u32[]{:S(2)}, u32[]{:S(2)}) %collective-permute-start.36) | collective-permute-done | bytes 131104 | tf_op jit(solution)/shard_map/ppermute | solution.py:254
  108.5 1.7 %shard_map.95 = (f32[64,512]{1,0:T(8,128)S(1)}, f32[64,512]{1,0:T(8,128)S(1)}, f32[64,512]{1,0:T(8,128)S(1)}, f32[64,512]{1,0:T(8,128)S(1)}) custom-call(s32[2]{0:T(128)S(1)} %pad_add_fusion.where, f32[256,512]{1,0:T(8,128)S(1)} %shard_map.94.refs_0_, f32[64,512]{1,0:T(8,128)S(1)} %add_add_fusion.1.refs_0_.refs_1_, ...), custom_call_target="tpu_custom_call" | custom-call | tf_op jit(solution)/shard_map/pallas_call | solution.py:227
  110.1 2.1 %collective-permute-start.45 = (f32[64,512]{1,0:T(8,128)S(1)}, f32[64,512]{1,0:T(8,128)S(1)}, u32[]{:S(2)}, u32[]{:S(2)}) collective-permute-start(f32[64,512]{1,0:T(8,128)S(1)} %get-tuple-element.41), channel_id=1, source_target_pairs={{0,2},{1,3},{2,0},{3,1},{4,6},{5,7},{6,4},{7,5},{8,10},{9,11},{10,... | collective-permute-start | bytes 393224 | tf_op jit(solution)/shard_map/ppermute | solution.py:254
  112.5 5.8 %collective-permute-done.37 = f32[64,512]{1,0:T(8,128)S(1)} collective-permute-done((f32[64,512]{1,0:T(8,128)S(1)}, f32[64,512]{1,0:T(8,128)S(1)}, u32[]{:S(2)}, u32[]{:S(2)}) %collective-permute-start.37) | collective-permute-done | bytes 131104 | tf_op jit(solution)/shard_map/ppermute | solution.py:254
  118.4 2.4 %collective-permute-start.47 = (f32[64,512]{1,0:T(8,128)S(1)}, f32[64,512]{1,0:T(8,128)S(1)}, u32[]{:S(2)}, u32[]{:S(2)}) collective-permute-start(f32[64,512]{1,0:T(8,128)S(1)} %get-tuple-element.43), channel_id=1, source_target_pairs={{0,3},{1,2},{2,1},{3,0},{4,7},{5,6},{6,5},{7,4},{8,11},{9,10},{10,... | collective-permute-start | bytes 393224 | tf_op jit(solution)/shard_map/ppermute | solution.py:254
  123.7 1.9 %collective-permute-done.47 = f32[64,512]{1,0:T(8,128)S(1)} collective-permute-done((f32[64,512]{1,0:T(8,128)S(1)}, f32[64,512]{1,0:T(8,128)S(1)}, u32[]{:S(2)}, u32[]{:S(2)}) %collective-permute-start.47) | collective-permute-done | bytes 131104 | tf_op jit(solution)/shard_map/ppermute | solution.py:254
  125.6 1.7 %collective-permute-start.48 = (f32[64,512]{1,0:T(8,128)S(1)}, f32[64,512]{1,0:T(8,128)S(1)}, u32[]{:S(2)}, u32[]{:S(2)}) collective-permute-start(f32[64,512]{1,0:T(8,128)S(1)} %add_add_fusion.refs_2_), channel_id=1, source_target_pairs={{0,2},{1,3},{2,0},{3,1},{4,6},{5,7},{6,4},{7,5},{8,10},{9,11},{10,... | collective-permute-start | bytes 393224 | tf_op jit(solution)/shard_map/ppermute | solution.py:254
  130.7 18.4 %shard_map.93.refs_0_ = f32[512,512]{1,0:T(8,128)S(1)} custom-call(s32[2]{0:T(128)S(1)} %pad_add_fusion.where, f32[64,512]{1,0:T(8,128)S(1)} %add.48.refs_0_, f32[64,512]{1,0:T(8,128)S(1)} %collective-permute-done.38.refs_1_, f32[64,512]{1,0:T(8,128)S(1)} %collective-permute-done.39.refs_2_, f32[64,512]{1,0:T(8,128)S(1)} %collective-permute-done.40.refs_3_, ...), custom_call_target="tpu_custom_call" | custom-call | tf_op jit(solution)/shard_map/pallas_call | solution.py:227
  149.1 3.5 %shard_map.96 = (f32[64,512]{1,0:T(8,128)}, f32[256,512]{1,0:T(8,128)}) custom-call(s32[2]{0:T(128)S(1)} %pad_add_fusion.where, f32[512,512]{1,0:T(8,128)S(1)} %shard_map.93.refs_0_, f32[64,512]{1,0:T(8,128)S(1)} %add_add_fusion.1.refs_0_.refs_1_, f32[64,512]{1,0:T(8,128)S(1)} %add_add_fusion.refs_2_, f32[64,512]{1,0:T(8,128)S(1)} %collective-permute-done.48.refs_3_, ...), custom_call_target="tpu_custom_call" | custom-call | tf_op jit(solution)/shard_map/pallas_call | solution.py:227
  (105 shorter events, 37.4 us)
Async XLA Ops:
  1.5 7.1 %collective-permute-start.3 = (bf16[64,512]{1,0:T(8,128)(2,1)S(1)}, bf16[64,512]{1,0:T(8,128)(2,1)S(1)}, u32[]{:S(2)}, u32[]{:S(2)}) collective-permute-start(bf16[64,512]{1,0:T(8,128)(2,1)S(1)} %constant_dynamic-slice_fusion), channel_id=1, source_target_pairs={{0,2},{1,3},{2,0},{3,1},{4,6},{5,7},{6,4},{7,5},{8,10},{9,11},{10,... | collective-permute-start | bytes 196616 | tf_op jit(solution)/shard_map/ppermute | solution.py:254
  13.2 8.4 %collective-permute-start.9 = (bf16[3,64,512]{2,1,0:T(8,128)(2,1)S(1)}, bf16[3,64,512]{2,1,0:T(8,128)(2,1)S(1)}, u32[]{:S(2)}, u32[]{:S(2)}) collective-permute-start(bf16[3,64,512]{2,1,0:T(8,128)(2,1)S(1)} %pad_maximum_fusion.refs_0_), channel_id=1, source_target_pairs={{0,16},{4,20},{8,24},{12,28},{16,0},{20,4},{24,8},{28,12},{1,17},{... | collective-permute-start | bytes 589832 | tf_op jit(solution)/shard_map/ppermute | solution.py:257
  14.8 7.8 %collective-permute-start.11 = (bf16[3,64,512]{2,1,0:T(8,128)(2,1)S(1)}, bf16[3,64,512]{2,1,0:T(8,128)(2,1)S(1)}, u32[]{:S(2)}, u32[]{:S(2)}) collective-permute-start(bf16[3,64,512]{2,1,0:T(8,128)(2,1)S(1)} %pad_maximum_fusion.refs_0_), channel_id=1, source_target_pairs={{0,24},{4,28},{8,16},{12,20},{16,8},{20,12},{24,0},{28,4},{1,25},{... | collective-permute-start | bytes 589832 | tf_op jit(solution)/shard_map/ppermute | solution.py:257
  16.2 7.5 %collective-permute-start.7 = (bf16[3,64,512]{2,1,0:T(8,128)(2,1)S(1)}, bf16[3,64,512]{2,1,0:T(8,128)(2,1)S(1)}, u32[]{:S(2)}, u32[]{:S(2)}) collective-permute-start(bf16[3,64,512]{2,1,0:T(8,128)(2,1)S(1)} %pad_maximum_fusion.refs_0_), channel_id=1, source_target_pairs={{0,8},{4,12},{8,0},{12,4},{16,24},{20,28},{24,16},{28,20},{1,9},{5... | collective-permute-start | bytes 589832 | tf_op jit(solution)/shard_map/ppermute | solution.py:257
  17.4 19.5 %collective-permute-start.6 = (bf16[3,64,512]{2,1,0:T(8,128)(2,1)S(1)}, bf16[3,64,512]{2,1,0:T(8,128)(2,1)S(1)}, u32[]{:S(2)}, u32[]{:S(2)}) collective-permute-start(bf16[3,64,512]{2,1,0:T(8,128)(2,1)S(1)} %pad_maximum_fusion.refs_0_), channel_id=1, source_target_pairs={{0,4},{4,0},{8,12},{12,8},{16,20},{20,16},{24,28},{28,24},{1,5},{5... | collective-permute-start | bytes 589832 | tf_op jit(solution)/shard_map/ppermute | solution.py:257
  21.6 17.1 %collective-permute-start.10 = (bf16[3,64,512]{2,1,0:T(8,128)(2,1)S(1)}, bf16[3,64,512]{2,1,0:T(8,128)(2,1)S(1)}, u32[]{:S(2)}, u32[]{:S(2)}) collective-permute-start(bf16[3,64,512]{2,1,0:T(8,128)(2,1)S(1)} %collective-permute-done.9.refs_4_), channel_id=1, source_target_pairs={{0,4},{4,0},{8,12},{12,8},{16,20},{20,16},{24,28},{28,24},{1,5},{5... | collective-permute-start | bytes 589832 | tf_op jit(solution)/shard_map/ppermute | solution.py:257
  22.6 17.9 %collective-permute-start.12 = (bf16[3,64,512]{2,1,0:T(8,128)(2,1)S(1)}, bf16[3,64,512]{2,1,0:T(8,128)(2,1)S(1)}, u32[]{:S(2)}, u32[]{:S(2)}) collective-permute-start(bf16[3,64,512]{2,1,0:T(8,128)(2,1)S(1)} %collective-permute-done.11.refs_6_), channel_id=1, source_target_pairs={{0,4},{4,0},{8,12},{12,8},{16,20},{20,16},{24,28},{28,24},{1,5},{5... | collective-permute-start | bytes 589832 | tf_op jit(solution)/shard_map/ppermute | solution.py:257
  23.8 17.6 %collective-permute-start.8 = (bf16[3,64,512]{2,1,0:T(8,128)(2,1)S(1)}, bf16[3,64,512]{2,1,0:T(8,128)(2,1)S(1)}, u32[]{:S(2)}, u32[]{:S(2)}) collective-permute-start(bf16[3,64,512]{2,1,0:T(8,128)(2,1)S(1)} %collective-permute-done.7.refs_2_), channel_id=1, source_target_pairs={{0,4},{4,0},{8,12},{12,8},{16,20},{20,16},{24,28},{28,24},{1,5},{5... | collective-permute-start | bytes 589832 | tf_op jit(solution)/shard_map/ppermute | solution.py:257
  27.2 9.7 %collective-permute-start.13 = (bf16[128,512]{1,0:T(8,128)(2,1)S(1)}, bf16[128,512]{1,0:T(8,128)(2,1)S(1)}, u32[]{:S(2)}, u32[]{:S(2)}) collective-permute-start(bf16[128,512]{1,0:T(8,128)(2,1)S(1)} %get-tuple-element.27.refs_3_), channel_id=1, source_target_pairs={{0,2},{1,3},{2,0},{3,1},{4,6},{5,7},{6,4},{7,5},{8,10},{9,11},{10,... | collective-permute-start | bytes 393224 | tf_op jit(solution)/shard_map/ppermute | solution.py:254
  36.9 8.9 %collective-permute-start.14 = (bf16[128,512]{1,0:T(8,128)(2,1)S(1)}, bf16[128,512]{1,0:T(8,128)(2,1)S(1)}, u32[]{:S(2)}, u32[]{:S(2)}) collective-permute-start(bf16[128,512]{1,0:T(8,128)(2,1)S(1)} %get-tuple-element.29.refs_5_), channel_id=1, source_target_pairs={{0,1},{1,0},{2,3},{3,2},{4,5},{5,4},{6,7},{7,6},{8,9},{9,8},{10,11... | collective-permute-start | bytes 393224 | tf_op jit(solution)/shard_map/ppermute | solution.py:254
  36.9 8.9 %collective-permute-start.15 = (bf16[128,512]{1,0:T(8,128)(2,1)S(1)}, bf16[128,512]{1,0:T(8,128)(2,1)S(1)}, u32[]{:S(2)}, u32[]{:S(2)}) collective-permute-start(bf16[128,512]{1,0:T(8,128)(2,1)S(1)} %get-tuple-element.31.refs_7_), channel_id=1, source_target_pairs={{0,3},{1,2},{2,1},{3,0},{4,7},{5,6},{6,5},{7,4},{8,11},{9,10},{10,... | collective-permute-start | bytes 393224 | tf_op jit(solution)/shard_map/ppermute | solution.py:254
  38.7 19.8 %collective-permute-start = (bf16[128,512]{1,0:T(8,128)(2,1)S(1)}, bf16[128,512]{1,0:T(8,128)(2,1)S(1)}, u32[]{:S(2)}, u32[]{:S(2)}) collective-permute-start(bf16[128,512]{1,0:T(8,128)(2,1)S(1)} %get-tuple-element.26.refs_2_), channel_id=1, source_target_pairs={{0,2},{1,3},{2,0},{3,1},{4,6},{5,7},{6,4},{7,5},{8,10},{9,11},{10,... | collective-permute-start | bytes 393224 | tf_op jit(solution)/shard_map/ppermute | solution.py:254
  40.4 18.1 %collective-permute-start.1 = (bf16[128,512]{1,0:T(8,128)(2,1)S(1)}, bf16[128,512]{1,0:T(8,128)(2,1)S(1)}, u32[]{:S(2)}, u32[]{:S(2)}) collective-permute-start(bf16[128,512]{1,0:T(8,128)(2,1)S(1)} %get-tuple-element.28.refs_4_), channel_id=1, source_target_pairs={{0,1},{1,0},{2,3},{3,2},{4,5},{5,4},{6,7},{7,6},{8,9},{9,8},{10,11... | collective-permute-start | bytes 393224 | tf_op jit(solution)/shard_map/ppermute | solution.py:254
  41.3 17.2 %collective-permute-start.2 = (bf16[128,512]{1,0:T(8,128)(2,1)S(1)}, bf16[128,512]{1,0:T(8,128)(2,1)S(1)}, u32[]{:S(2)}, u32[]{:S(2)}) collective-permute-start(bf16[128,512]{1,0:T(8,128)(2,1)S(1)} %get-tuple-element.30.refs_6_), channel_id=1, source_target_pairs={{0,3},{1,2},{2,1},{3,0},{4,7},{5,6},{6,5},{7,4},{8,11},{9,10},{10,... | collective-permute-start | bytes 393224 | tf_op jit(solution)/shard_map/ppermute | solution.py:254
  46.2 19.4 %collective-permute-start.17 = (bf16[128,512]{1,0:T(8,128)(2,1)S(1)}, bf16[128,512]{1,0:T(8,128)(2,1)S(1)}, u32[]{:S(2)}, u32[]{:S(2)}) collective-permute-start(bf16[128,512]{1,0:T(8,128)(2,1)S(1)} %shard_map.90.refs_2_), channel_id=1, source_target_pairs={{0,2},{1,3},{2,0},{3,1},{4,6},{5,7},{6,4},{7,5},{8,10},{9,11},{10,... | collective-permute-start | bytes 393224 | tf_op jit(solution)/shard_map/ppermute | solution.py:254
  59.0 9.7 %collective-permute-start.16 = (bf16[128,512]{1,0:T(8,128)(2,1)S(1)}, bf16[128,512]{1,0:T(8,128)(2,1)S(1)}, u32[]{:S(2)}, u32[]{:S(2)}) collective-permute-start(bf16[128,512]{1,0:T(8,128)(2,1)S(1)} %shard_map.89.refs_1_), channel_id=1, source_target_pairs={{0,2},{1,3},{2,0},{3,1},{4,6},{5,7},{6,4},{7,5},{8,10},{9,11},{10,... | collective-permute-start | bytes 393224 | tf_op jit(solution)/shard_map/ppermute | solution.py:254
  62.7 7.6 %collective-permute-start.19 = (bf16[128,512]{1,0:T(8,128)(2,1)S(1)}, bf16[128,512]{1,0:T(8,128)(2,1)S(1)}, u32[]{:S(2)}, u32[]{:S(2)}) collective-permute-start(bf16[128,512]{1,0:T(8,128)(2,1)S(1)} %shard_map.90.refs_2_), channel_id=1, source_target_pairs={{0,1},{1,0},{2,3},{3,2},{4,5},{5,4},{6,7},{7,6},{8,9},{9,8},{10,11... | collective-permute-start | bytes 393224 | tf_op jit(solution)/shard_map/ppermute | solution.py:254
  62.7 10.4 %collective-permute-start.18 = (bf16[128,512]{1,0:T(8,128)(2,1)S(1)}, bf16[128,512]{1,0:T(8,128)(2,1)S(1)}, u32[]{:S(2)}, u32[]{:S(2)}) collective-permute-start(bf16[128,512]{1,0:T(8,128)(2,1)S(1)} %shard_map.89.refs_1_), channel_id=1, source_target_pairs={{0,1},{1,0},{2,3},{3,2},{4,5},{5,4},{6,7},{7,6},{8,9},{9,8},{10,11... | collective-permute-start | bytes 393224 | tf_op jit(solution)/shard_map/ppermute | solution.py:254
  65.7 10.2 %collective-permute-start.21 = (bf16[128,512]{1,0:T(8,128)(2,1)S(1)}, bf16[128,512]{1,0:T(8,128)(2,1)S(1)}, u32[]{:S(2)}, u32[]{:S(2)}) collective-permute-start(bf16[128,512]{1,0:T(8,128)(2,1)S(1)} %collective-permute-done.17.refs_4_), channel_id=1, source_target_pairs={{0,1},{1,0},{2,3},{3,2},{4,5},{5,4},{6,7},{7,6},{8,9},{9,8},{10,11... | collective-permute-start | bytes 393224 | tf_op jit(solution)/shard_map/ppermute | solution.py:254
  68.7 8.6 %collective-permute-start.20 = (bf16[128,512]{1,0:T(8,128)(2,1)S(1)}, bf16[128,512]{1,0:T(8,128)(2,1)S(1)}, u32[]{:S(2)}, u32[]{:S(2)}) collective-permute-start(bf16[128,512]{1,0:T(8,128)(2,1)S(1)} %collective-permute-done.16.refs_3_), channel_id=1, source_target_pairs={{0,1},{1,0},{2,3},{3,2},{4,5},{5,4},{6,7},{7,6},{8,9},{9,8},{10,11... | collective-permute-start | bytes 393224 | tf_op jit(solution)/shard_map/ppermute | solution.py:254
  81.3 8.1 %collective-permute-start.26 = (f32[64,512]{1,0:T(8,128)S(1)}, f32[64,512]{1,0:T(8,128)S(1)}, u32[]{:S(2)}, u32[]{:S(2)}) collective-permute-start(f32[64,512]{1,0:T(8,128)S(1)} %add.43), channel_id=1, source_target_pairs={{0,16},{4,20},{8,24},{12,28},{16,0},{20,4},{24,8},{28,12},{1,17},{... | collective-permute-start | bytes 393224 | tf_op jit(solution)/shard_map/ppermute | solution.py:257
  83.0 6.5 %collective-permute-start.28 = (f32[64,512]{1,0:T(8,128)S(1)}, f32[64,512]{1,0:T(8,128)S(1)}, u32[]{:S(2)}, u32[]{:S(2)}) collective-permute-start(f32[64,512]{1,0:T(8,128)S(1)} %add.45), channel_id=1, source_target_pairs={{0,24},{4,28},{8,16},{12,20},{16,8},{20,12},{24,0},{28,4},{1,25},{... | collective-permute-start | bytes 393224 | tf_op jit(solution)/shard_map/ppermute | solution.py:257
  90.8 7.2 %collective-permute-start.32 = (f32[64,512]{1,0:T(8,128)S(1)}, f32[64,512]{1,0:T(8,128)S(1)}, u32[]{:S(2)}, u32[]{:S(2)}) collective-permute-start(f32[64,512]{1,0:T(8,128)S(1)} %add_add_fusion.1.refs_0_.refs_1_), channel_id=1, source_target_pairs={{0,16},{4,20},{8,24},{12,28},{16,0},{20,4},{24,8},{28,12},{1,17},{... | collective-permute-start | bytes 393224 | tf_op jit(solution)/shard_map/ppermute | solution.py:257
  106.6 11.7 %collective-permute-start.37 = (f32[64,512]{1,0:T(8,128)S(1)}, f32[64,512]{1,0:T(8,128)S(1)}, u32[]{:S(2)}, u32[]{:S(2)}) collective-permute-start(f32[64,512]{1,0:T(8,128)S(1)} %add.47), channel_id=1, source_target_pairs={{0,2},{1,3},{2,0},{3,1},{4,6},{5,7},{6,4},{7,5},{8,10},{9,11},{10,... | collective-permute-start | bytes 393224 | tf_op jit(solution)/shard_map/ppermute | solution.py:254
  110.1 11.8 %collective-permute-start.45 = (f32[64,512]{1,0:T(8,128)S(1)}, f32[64,512]{1,0:T(8,128)S(1)}, u32[]{:S(2)}, u32[]{:S(2)}) collective-permute-start(f32[64,512]{1,0:T(8,128)S(1)} %get-tuple-element.41), channel_id=1, source_target_pairs={{0,2},{1,3},{2,0},{3,1},{4,6},{5,7},{6,4},{7,5},{8,10},{9,11},{10,... | collective-permute-start | bytes 393224 | tf_op jit(solution)/shard_map/ppermute | solution.py:254
  112.2 11.0 %collective-permute-start.46 = (f32[64,512]{1,0:T(8,128)S(1)}, f32[64,512]{1,0:T(8,128)S(1)}, u32[]{:S(2)}, u32[]{:S(2)}) collective-permute-start(f32[64,512]{1,0:T(8,128)S(1)} %get-tuple-element.42), channel_id=1, source_target_pairs={{0,1},{1,0},{2,3},{3,2},{4,5},{5,4},{6,7},{7,6},{8,9},{9,8},{10,11... | collective-permute-start | bytes 393224 | tf_op jit(solution)/shard_map/ppermute | solution.py:254
  118.4 7.2 %collective-permute-start.47 = (f32[64,512]{1,0:T(8,128)S(1)}, f32[64,512]{1,0:T(8,128)S(1)}, u32[]{:S(2)}, u32[]{:S(2)}) collective-permute-start(f32[64,512]{1,0:T(8,128)S(1)} %get-tuple-element.43), channel_id=1, source_target_pairs={{0,3},{1,2},{2,1},{3,0},{4,7},{5,6},{6,5},{7,4},{8,11},{9,10},{10,... | collective-permute-start | bytes 393224 | tf_op jit(solution)/shard_map/ppermute | solution.py:254
  120.8 7.8 %collective-permute-start.41 = (f32[64,512]{1,0:T(8,128)S(1)}, f32[64,512]{1,0:T(8,128)S(1)}, u32[]{:S(2)}, u32[]{:S(2)}) collective-permute-start(f32[64,512]{1,0:T(8,128)S(1)} %add.48.refs_0_), channel_id=1, source_target_pairs={{0,16},{4,20},{8,24},{12,28},{16,0},{20,4},{24,8},{28,12},{1,17},{... | collective-permute-start | bytes 393224 | tf_op jit(solution)/shard_map/ppermute | solution.py:257
  121.9 6.6 %collective-permute-start.43 = (f32[64,512]{1,0:T(8,128)S(1)}, f32[64,512]{1,0:T(8,128)S(1)}, u32[]{:S(2)}, u32[]{:S(2)}) collective-permute-start(f32[64,512]{1,0:T(8,128)S(1)} %add.48.refs_0_), channel_id=1, source_target_pairs={{0,24},{4,28},{8,16},{12,20},{16,8},{20,12},{24,0},{28,4},{1,25},{... | collective-permute-start | bytes 393224 | tf_op jit(solution)/shard_map/ppermute | solution.py:257
  125.6 23.4 %collective-permute-start.48 = (f32[64,512]{1,0:T(8,128)S(1)}, f32[64,512]{1,0:T(8,128)S(1)}, u32[]{:S(2)}, u32[]{:S(2)}) collective-permute-start(f32[64,512]{1,0:T(8,128)S(1)} %add_add_fusion.refs_2_), channel_id=1, source_target_pairs={{0,2},{1,3},{2,0},{3,1},{4,6},{5,7},{6,4},{7,5},{8,10},{9,11},{10,... | collective-permute-start | bytes 393224 | tf_op jit(solution)/shard_map/ppermute | solution.py:254
  129.1 20.0 %collective-permute-start.49 = (f32[64,512]{1,0:T(8,128)S(1)}, f32[64,512]{1,0:T(8,128)S(1)}, u32[]{:S(2)}, u32[]{:S(2)}) collective-permute-start(f32[64,512]{1,0:T(8,128)S(1)} %add_add_fusion.refs_2_), channel_id=1, source_target_pairs={{0,1},{1,0},{2,3},{3,2},{4,5},{5,4},{6,7},{7,6},{8,9},{9,8},{10,11... | collective-permute-start | bytes 393224 | tf_op jit(solution)/shard_map/ppermute | solution.py:254
  129.1 20.0 %collective-permute-start.50 = (f32[64,512]{1,0:T(8,128)S(1)}, f32[64,512]{1,0:T(8,128)S(1)}, u32[]{:S(2)}, u32[]{:S(2)}) collective-permute-start(f32[64,512]{1,0:T(8,128)S(1)} %add_add_fusion.refs_2_), channel_id=1, source_target_pairs={{0,3},{1,2},{2,1},{3,0},{4,7},{5,6},{6,5},{7,4},{8,11},{9,10},{10,... | collective-permute-start | bytes 393224 | tf_op jit(solution)/shard_map/ppermute | solution.py:254
  (25 other events, 130.3 us)
where the time goes:
time: 153 us
  waiting for transfers between devices  66.6 us (44%)
  starting transfers between devices  51.1 us (33%)
  Pallas kernels  29.6 us (19%)
  local copies, waits for them, and re-layouts  3.47 us (2%)
  between operations  1.53 us (1%)
    ppermute x23, waiting for transfers between devices, along(): return lax.ppermute(x, 'vocab', [(a, a ^ place) for a in range(n_vocab)])  46.8 us
    ppermute x23, starting transfers between devices, along(): return lax.ppermute(x, 'vocab', [(a, a ^ place) for a in range(n_vocab)])  35.6 us
    pallas_call x11, Pallas kernels, call(): pl.pallas_call(kernel, out_shape=outs, in_specs=[smem] * len(scalars) + [...  29.6 us
    ppermute x28, waiting for transfers between devices, across(): return lax.ppermute(x, 'doc', [(a, a ^ place) for a in range(n_doc)])  19.8 us
    ppermute x28, starting transfers between devices, across(): return lax.ppermute(x, 'doc', [(a, a ^ place) for a in range(n_doc)])  15.6 us
  transfers between devices with their start and end apart: 51, of which 27 were waited for; matrix products, arithmetic and copies ran while one was open for 0% of the time, Pallas kernels for 15%

commit v1 on v0

--- a/solution.py
+++ b/solution.py
@@ -8,6 +8,7 @@
 
 ROW_TILES = 8
 PANEL = 32
+AHEAD = 10
 TILE = 128
 CORES = 2
 HALVES = 2
@@ -25,43 +26,79 @@
     )
 
 
-def invert_factor(work):
+def invert_factor(work, first, last):
     tiles = work.shape[0] // TILE
     chunks = PANEL // 8
     panels = TILE // PANEL
     sub_id = lax.broadcasted_iota(jnp.int32, (8, TILE), 0)
     lane_id = lax.broadcasted_iota(jnp.int32, (8, TILE), 1)
+    square_lanes = lax.broadcasted_iota(jnp.int32, (TILE, TILE), 1)
 
     def block(o, carry):
         base = pl.multiple_of(o * TILE, TILE)
+
+        def earlier(b, inner):
+            above_at = pl.multiple_of(b * TILE, TILE)
+            left = work[pl.ds(above_at, TILE), pl.ds(base, TILE)]
+            update = dot(left, work[pl.ds(above_at, TILE), :], ((0,), (0,)), precise)
+            work[pl.ds(base, TILE), :] = work[pl.ds(base, TILE), :] - update
+            work[pl.ds(above_at, TILE), pl.ds(base, TILE)] = jnp.zeros((TILE, TILE), f32)
+            return inner
+
+        lax.fori_loop(0, o, earlier, 0)
         for s in range(panels):
             lo = s * PANEL
             at = base + lo
-            own = [work[pl.ds(at + 8 * r, 8), pl.ds(base, TILE)] for r in range(chunks)]
-            col = [[None] * chunks for _ in range(PANEL)]
-            for l in range(PANEL):
-                for r in range(l // 8, chunks):
-                    col[l][r] = jnp.broadcast_to(own[r][:, lo + l : lo + l + 1], (8, TILE))
-            in_panel = (lane_id >= lo) & (lane_id < lo + PANEL)
+            if s > 0:
+                left = work[pl.ds(base, TILE), pl.ds(base, TILE)].T[lo : lo + PANEL]
+                left = jnp.where(square_lanes[:PANEL] < lo, left, 0.0)
+                update = dot(left, work[pl.ds(base, TILE), :], ((1,), (0,)), precise)
+                above = work[pl.ds(base, lo), pl.ds(base, TILE)]
+                gone = (square_lanes[:lo] >= lo) & (square_lanes[:lo] < lo + PANEL)
+                work[pl.ds(base, lo), pl.ds(base, TILE)] = jnp.where(gone, 0.0, above)
             rows = []
             for r in range(chunks):
-                eye = (lane_id == lo + 8 * r + sub_id).astype(f32)
                 line = []
                 for t in range(tiles):
                     old = work[pl.ds(at + 8 * r, 8), t * TILE : (t + 1) * TILE]
-                    line.append(jnp.where(in_panel & (o == t), eye, old))
+                    if s > 0:
+                        old = jnp.where((lane_id < lo) & (o == t), 0.0, old)
+                        old = old - update[8 * r : 8 * r + 8, t * TILE : (t + 1) * TILE]
+                    line.append(old)
                 rows.append(line)
+            own = []
+            for r in range(chunks):
+                mine = rows[r][0]
+                for t in range(1, tiles):
+                    mine = jnp.where(o == t, rows[r][t], mine)
+                own.append(mine)
+            in_panel = (lane_id >= lo) & (lane_id < lo + PANEL)
+            for r in range(chunks):
+                eye = (lane_id == lo + 8 * r + sub_id).astype(f32)
+                for t in range(tiles):
+                    rows[r][t] = jnp.where(in_panel & (o == t), eye, rows[r][t])
+
+            def column(l):
+                return [
+                    jnp.broadcast_to(own[r][:, lo + l : lo + l + 1], (8, TILE)) if r >= l // 8 else None
+                    for r in range(chunks)
+                ]
+
+            col = {l: column(l) for l in range(AHEAD)}
             for k in range(PANEL):
                 kr, ks = k // 8, k % 8
                 pivot = jnp.broadcast_to(col[k][kr][ks : ks + 1, :], (8, TILE))
                 q = lax.rsqrt(pivot)
-                lcol = [None] * chunks
-                for r in range(kr, chunks):
-                    lcol[r] = col[k][r] * q
-                for l in range(k + 1, PANEL):
+                lcol = [col[k][r] * q if r >= kr else None for r in range(chunks)]
+                for l in range(k + 1, min(k + AHEAD, PANEL)):
                     e = jnp.broadcast_to(lcol[l // 8][l % 8 : l % 8 + 1, :], (8, TILE))
                     for r in range(l // 8, chunks):
                         col[l][r] = col[l][r] - lcol[r] * e
+                if k + AHEAD < PANEL:
+                    rk = jnp.broadcast_to(own[kr][ks : ks + 1, :], (8, TILE)) * q
+                    for r in range(kr, chunks):
+                        own[r] = own[r] - lcol[r] * rk
+                    col[k + AHEAD] = column(k + AHEAD)
                 below = jnp.where(sub_id > ks, lcol[kr], 0.0)
                 for t in range(tiles):
                     rk = jnp.broadcast_to(rows[kr][t][ks : ks + 1, :], (8, TILE)) * q
@@ -71,51 +108,24 @@
             for r in range(chunks):
                 for t in range(tiles):
                     work[pl.ds(at + 8 * r, 8), t * TILE : (t + 1) * TILE] = rows[r][t]
-            if s + 1 < panels:
-                left = work[pl.ds(at, PANEL), pl.ds(base, TILE)]
-                full = work[pl.ds(at, PANEL), :]
-                update = dot(left, full, ((0,), (0,)), precise)
-                first = lo + PANEL
-                count = TILE - first
-                lanes = lax.broadcasted_iota(jnp.int32, (count, TILE), 1)
-                gone = (lanes >= lo) & (lanes < lo + PANEL)
-                for t in range(tiles):
-                    span = slice(t * TILE, (t + 1) * TILE)
-                    old = work[pl.ds(base + first, count), span]
-                    old = jnp.where(gone & (o == t), 0.0, old)
-                    work[pl.ds(base + first, count), span] = old - update[first:, span]
-        square = work[pl.ds(base, TILE), pl.ds(base, TILE)]
-        lower = lax.broadcasted_iota(jnp.int32, (TILE, TILE), 0) >= lax.broadcasted_iota(
-            jnp.int32, (TILE, TILE), 1
-        )
-        work[pl.ds(base, TILE), pl.ds(base, TILE)] = jnp.where(lower, square, 0.0)
-
-        def later(b, inner):
-            below_at = pl.multiple_of(b * TILE, TILE)
-            left = work[pl.ds(base, TILE), pl.ds(below_at, TILE)]
-            update = dot(left, work[pl.ds(base, TILE), :], ((0,), (0,)), precise)
-            work[pl.ds(below_at, TILE), pl.ds(base, TILE)] = jnp.zeros((TILE, TILE), f32)
-            work[pl.ds(below_at, TILE), :] = work[pl.ds(below_at, TILE), :] - update
-            return inner
-
-        lax.fori_loop(o + 1, tiles, later, 0)
         return carry
 
-    lax.fori_loop(0, tiles, block, 0)
-
-
-def dense_kernel(where, halves, places, at_rows, at_columns, used, tiles, *refs):
+    lax.fori_loop(first, last, block, 0)
+
+
+def dense_kernel(where, halves, places, tiles, *refs):
     outs, dense = refs[:-1], refs[-1]
     rows = dense.shape[0] // len(outs)
+    slots = tiles.shape[0]
     dense[...] = jnp.zeros_like(dense)
 
     def place(s, carry):
-        r = pl.multiple_of(at_rows[0, s] * TILE, TILE)
-        c = pl.multiple_of(at_columns[0, s] * TILE, TILE)
+        r = pl.multiple_of(where[3 + s] * TILE, TILE)
+        c = pl.multiple_of(where[3 + slots + s] * TILE, TILE)
         dense[pl.ds(r, TILE), pl.ds(c, TILE)] = tiles[s]
         return carry
 
-    lax.fori_loop(0, used[0, 0], place, 0)
+    lax.fori_loop(0, where[2], place, 0)
     for i, out in enumerate(outs):
         block = lax.bitwise_xor(where[0], places[i // halves]) * halves + i % halves
         out[...] = dense[pl.ds(pl.multiple_of(block * rows, rows), rows), :]
@@ -164,11 +174,20 @@
     rows = pieces[0].shape[0]
     for i, piece in enumerate(pieces):
         back[i * rows : (i + 1) * rows, :] = piece[...]
-    share = gram.shape[0]
-    start = where[1] * share
-    tile_at = pl.multiple_of(start // TILE * TILE, TILE)
-    product[...] = dot(back[:, pl.ds(tile_at, TILE)], back[...], ((0,), (0,)), precise)
-    gram[...] = product[pl.ds(pl.multiple_of(start - tile_at, share), share), :]
+    width = back.shape[1]
+    band = gram.shape[0]
+    bands = width // band
+    halves = []
+    for half, index in enumerate((where[1], bands - 1 - where[1])):
+        start = index * band
+        tile_at = pl.multiple_of(start // TILE * TILE, TILE)
+        product[half] = dot(back[:, pl.ds(tile_at, TILE)], back[...], ((0,), (0,)), precise)
+        halves.append(product[half, pl.ds(pl.multiple_of(start - tile_at, band), band), :])
+    lead = where[1] * band // PANEL * PANEL
+    turned = pltpu.roll(halves[1], lead, 1)
+    lanes = lax.broadcasted_iota(jnp.int32, (band, width), 1)
+    gram[:, :width] = jnp.where(lanes >= lead, halves[0], turned)
+    gram[:, width:] = turned[:, width - TILE :]
 
 
 def query_dense_kernel(tiles, values, out):
@@ -180,7 +199,7 @@
         out[:, c * TILE : (c + 1) * TILE] = total
 
 
-def query_kernel(where, places, v_places, dense, *refs):
+def query_kernel(where, places, dense, *refs):
     pieces = refs[: len(places)]
     outs = refs[len(places) : -2]
     back, full = refs[-2:]
@@ -189,34 +208,51 @@
         at = pl.multiple_of(lax.bitwise_xor(where[1], place) * height, height)
         back[pl.ds(at, height), :] = piece[...]
     full[...] = dot(dense[...], back[...], ((1,), (0,)), precise)
-    rows = outs[0].shape[0]
-    for out, place in zip(outs, v_places):
+    rows = outs[0].shape[1]
+    for place in range(2 * outs[0].shape[0]):
         at = pl.multiple_of(lax.bitwise_xor(where[0], place) * rows, rows)
-        out[...] = full[pl.ds(at, rows), :]
+        outs[place % 2][place // 2] = full[pl.ds(at, rows), :]
 
 
 def factor_kernel(where, places, scale, *refs):
-    pieces, out, work = refs[: len(places)], refs[-2], refs[-1]
-    rows = pieces[0].shape[0]
+    pieces, work = refs[: len(places)], refs[-1]
+    n = work.shape[0]
+    band = pieces[0].shape[0]
+    bands = n // band
+    lanes = lax.broadcasted_iota(jnp.int32, (band, n), 1)
     for piece, place in zip(pieces, places):
-        at = pl.multiple_of(lax.bitwise_xor(where[1], place) * rows, rows)
-        work[pl.ds(at, rows), :] = piece[...] * scale
-    invert_factor(work)
-    n = work.shape[0]
-    lower = lax.broadcasted_iota(jnp.int32, (n, n), 0) >= lax.broadcasted_iota(jnp.int32, (n, n), 1)
-    out[...] = jnp.where(lower, work[...], 0.0)
-
-
-def output_kernel(where, v_places, *refs):
+        index = lax.bitwise_xor(where[1], place)
+        lead = index * band // PANEL * PANEL
+        packed = piece[:, :n] * scale
+        tail = piece[:, n:] * scale
+        first = jnp.where(lanes >= lead, packed, 0.0)
+        work[pl.ds(pl.multiple_of(index * band, band), band), :] = first
+        whole = jnp.concatenate([packed[:, : n - TILE], tail], axis=1)
+        whole = jnp.where((lanes < lead) | (lanes >= n - PANEL), whole, 0.0)
+        second = pltpu.roll(whole, lax.rem(n - lead, n), 1)
+        work[pl.ds(pl.multiple_of((bands - 1 - index) * band, band), band), :] = second
+    invert_factor(work, 0, n // TILE // 2)
+
+
+def finish_kernel(begun, work):
+    work[...] = begun[...]
+    tiles = work.shape[0] // TILE
+    invert_factor(work, tiles // 2, tiles)
+
+
+def output_kernel(where, held_places, *refs):
     inverse, own = refs[0], refs[1]
-    coords = refs[2 : 2 + len(v_places)]
-    basis, projections, full = refs[2 + len(v_places) :]
-    rows = coords[0].shape[0]
-    for piece, place in zip(coords, v_places):
-        at = pl.multiple_of(lax.bitwise_xor(where[0], place) * rows, rows)
-        full[pl.ds(at, rows), :] = piece[...]
-    basis[...] = dot(own[...], inverse[...], ((1,), (1,)), precise)
-    raw = dot(full[...], inverse[...], ((1,), (1,)), precise)
+    coords = refs[2 : 2 + len(held_places)]
+    basis, projections, full = refs[2 + len(held_places) :]
+    share, rows = own.shape[0], coords[0].shape[1]
+    full[:share, :] = own[...]
+    for piece, pair in zip(coords, held_places):
+        for i, place in enumerate(pair):
+            at = pl.multiple_of(lax.bitwise_xor(where[0], place) * rows, rows)
+            full[pl.ds(share + at, rows), :] = piece[i]
+    product = dot(full[...], inverse[...], ((1,), (1,)), precise)
+    basis[...] = product[:share]
+    raw = product[share:]
     mean = jnp.sum(raw * raw, axis=1, keepdims=True) * (1.0 / raw.shape[1])
     projections[...] = raw * lax.rsqrt(mean + 1e-06)
 
@@ -237,7 +273,9 @@
 def work(tile_values, tile_rows, tile_columns, counts, sketch, query_tiles, query_values):
     n_doc, n_vocab = lax.axis_size("doc"), lax.axis_size("vocab")
     doc, vocab = lax.axis_index("doc"), lax.axis_index("vocab")
-    where = jnp.stack([vocab, doc]).astype(jnp.int32)
+    where = jnp.concatenate(
+        [jnp.stack([vocab, doc]).astype(jnp.int32), counts[0], tile_rows[0, 0], tile_columns[0, 0]]
+    )
     chips = n_doc // CORES
     edge = tile_values.shape[3]
     terms, width = sketch.shape
@@ -275,7 +313,7 @@
         lambda where, *refs: dense_kernel(where, HALVES, v_places, *refs),
         [jax.ShapeDtypeStruct((rows, terms), bf16)] * (n_vocab * HALVES),
         [pltpu.VMEM((documents, terms), bf16)],
-        [where, tile_rows[0], tile_columns[0], counts],
+        [where],
         [tile_values[0, 0]],
     )
     own_terms = lax.dynamic_slice_in_dim(sketch, doc * share, share, 0)
@@ -324,43 +362,50 @@
     for m in range(1, chips):
         own_back = own_back + across(paired[m], CORES * m)
     back_pieces = spread(own_back)
-    gram_share = width // n_doc
+    band = width // n_doc // 2
     gram_rows = call(
         lambda where, *refs: gram_kernel(where, places, *refs),
-        jax.ShapeDtypeStruct((gram_share, width), f32),
-        [pltpu.VMEM((terms, width), f32), pltpu.VMEM((TILE, width), f32)],
+        jax.ShapeDtypeStruct((band, width + TILE), f32),
+        [pltpu.VMEM((terms, width), f32), pltpu.VMEM((2, TILE, width), f32)],
         [where],
         back_pieces,
     )
     for bit in reversed(bits):
         gram_rows = gram_rows + along(gram_rows, bit)
     query_rows = queries // n_vocab
-    query_parts = call(
-        lambda where, *refs: query_kernel(where, places, v_places, *refs),
-        [jax.ShapeDtypeStruct((query_rows, width), f32)] * n_vocab,
+    even, odd = call(
+        lambda where, *refs: query_kernel(where, places, *refs),
+        [jax.ShapeDtypeStruct((n_vocab // 2, query_rows, width), f32)] * 2,
         [pltpu.VMEM((terms, width), f32), pltpu.VMEM((queries, width), f32)],
         [where],
         [query_dense, *back_pieces],
     )
+    partial_query = even + along(odd, 1)
     gram_pieces = spread(gram_rows)
-    own_query = query_parts[0]
-    for i in range(1, n_vocab):
-        own_query = own_query + along(query_parts[i], v_places[i])
-    coords = [own_query] + [along(own_query, place) for place in v_places[1:]]
-    inverse = call(
+    bit, top = 2, n_vocab // 2
+    while bit < top:
+        partial_query = partial_query[0::2] + along(partial_query[1::2], bit)
+        bit *= 2
+    own_query = partial_query + along(partial_query[::-1], top)
+    begun = call(
         lambda where, *refs: factor_kernel(where, places, 1.0 / (terms * n_vocab), *refs),
         jax.ShapeDtypeStruct((width, width), f32),
-        [pltpu.VMEM((width, width), f32)],
+        [],
         [where],
         gram_pieces,
     )
+    coords, held_places = [own_query], [(0, top)]
+    for bit in bits[1:]:
+        coords += [along(piece, bit) for piece in coords]
+        held_places += [(near | bit, far | bit) for near, far in held_places]
+    inverse = call(finish_kernel, jax.ShapeDtypeStruct((width, width), f32), [], [], [begun])
     basis, projections = call(
-        lambda where, *refs: output_kernel(where, v_places, *refs),
+        lambda where, *refs: output_kernel(where, held_places, *refs),
         [
             jax.ShapeDtypeStruct((share, width), f32),
             jax.ShapeDtypeStruct((queries, width), f32),
         ],
-        [pltpu.VMEM((queries, width), f32)],
+        [pltpu.VMEM((share + queries, width), f32)],
         [where],
         [inverse, own_back, *coords],
         keep=False,

time: 153 us -> 160 us (1.046)
  waiting for transfers between devices: 66.6 us -> 80.3 us
  starting transfers between devices: 51.1 us -> 47.6 us
  Pallas kernels: 29.6 us -> 27.1 us
    ppermute x23 -> x20, waiting for transfers between devices: 46.8 us -> 57.4 us  [along(): return lax.ppermute(x, 'vocab', [(a, a ^ place) for a in range(n_vocab)])]
    ppermute x23 -> x20, starting transfers between devices: 35.6 us -> 31.3 us  [along(): return lax.ppermute(x, 'vocab', [(a, a ^ place) for a in range(n_vocab)])]
    ppermute x28, waiting for transfers between devices: 19.8 us -> 23 us  [across(): return lax.ppermute(x, 'doc', [(a, a ^ place) for a in range(n_doc)])]
    pallas_call x11 -> x12, Pallas kernels: 29.6 us -> 27.1 us  [call(): pl.pallas_call(kernel, out_shape=outs, in_specs=[smem] * len(scalars) + [...]
  transfers between devices with their start and end apart: 51 -> 48, of which waited for: 27 -> 28; matrix products, arithmetic and copies ran while one was open for 0% -> 1% of each run, Pallas kernels for 15% -> 13%
where the time goes in v1:
time: 160 us
  waiting for transfers between devices  80.3 us (50%)
  starting transfers between devices  47.6 us (30%)
  Pallas kernels  27.1 us (17%)
  local copies, waits for them, and re-layouts  2.94 us (2%)
    ppermute x20, waiting for transfers between devices, along(): return lax.ppermute(x, 'vocab', [(a, a ^ place) for a in range(n_vocab)])  57.4 us
    ppermute x20, starting transfers between devices, along(): return lax.ppermute(x, 'vocab', [(a, a ^ place) for a in range(n_vocab)])  31.3 us
    pallas_call x12, Pallas kernels, call(): pl.pallas_call(kernel, out_shape=outs, in_specs=[smem] * len(scalars) + [...  27.1 us
    ppermute x28, waiting for transfers between devices, across(): return lax.ppermute(x, 'doc', [(a, a ^ place) for a in range(n_doc)])  23 us
    ppermute x28, starting transfers between devices, across(): return lax.ppermute(x, 'doc', [(a, a ^ place) for a in range(n_doc)])  16.4 us
  transfers between devices with their start and end apart: 48, of which 28 were waited for; matrix products, arithmetic and copies ran while one was open for 1% of the time, Pallas kernels for 13%

profile of v1, /device:TPU:0, one launch (start us, length us, event | category | flops | bytes accessed | tf_op | source)
XLA Modules:
  0.0 159.8 jit_solution(15723834172524078520)
XLA Ops:
  1.5 4.1 %collective-permute-start.3 = (bf16[64,512]{1,0:T(8,128)(2,1)S(1)}, bf16[64,512]{1,0:T(8,128)(2,1)S(1)}, u32[]{:S(2)}, u32[]{:S(2)}) collective-permute-start(bf16[64,512]{1,0:T(8,128)(2,1)S(1)} %constant_dynamic-slice_fusion), channel_id=1, source_target_pairs={{0,2},{1,3},{2,0},{3,1},{4,6},{5,7},{6,4},{7,5},{8,10},{9,11},{10,... | collective-permute-start | bytes 196616 | tf_op jit(solution)/shard_map/ppermute | solution.py:292
  9.8 3.4 %collective-permute-done.5 = bf16[64,512]{1,0:T(8,128)(2,1)S(1)} collective-permute-done((bf16[64,512]{1,0:T(8,128)(2,1)S(1)}, bf16[64,512]{1,0:T(8,128)(2,1)S(1)}, u32[]{:S(2)}, u32[]{:S(2)}) %collective-permute-start.5) | collective-permute-done | bytes 65568 | tf_op jit(solution)/shard_map/ppermute | solution.py:292
  16.8 4.9 %collective-permute-done.9.refs_4_ = bf16[3,64,512]{2,1,0:T(8,128)(2,1)S(1)} collective-permute-done((bf16[3,64,512]{2,1,0:T(8,128)(2,1)S(1)}, bf16[3,64,512]{2,1,0:T(8,128)(2,1)S(1)}, u32[]{:S(2)}, u32[]{:S(2)}) %collective-permute-start.9) | collective-permute-done | bytes 196640 | tf_op jit(solution)/shard_map/ppermute | solution.py:295
  27.3 2.6 %collective-permute-start.13 = (bf16[128,512]{1,0:T(8,128)(2,1)S(1)}, bf16[128,512]{1,0:T(8,128)(2,1)S(1)}, u32[]{:S(2)}, u32[]{:S(2)}) collective-permute-start(bf16[128,512]{1,0:T(8,128)(2,1)S(1)} %get-tuple-element.25.refs_3_), channel_id=1, source_target_pairs={{0,2},{1,3},{2,0},{3,1},{4,6},{5,7},{6,4},{7,5},{8,10},{9,11},{10,... | collective-permute-start | bytes 393224 | tf_op jit(solution)/shard_map/ppermute | solution.py:292
  29.9 7.0 %collective-permute-done.13.refs_1_ = bf16[128,512]{1,0:T(8,128)(2,1)S(1)} collective-permute-done((bf16[128,512]{1,0:T(8,128)(2,1)S(1)}, bf16[128,512]{1,0:T(8,128)(2,1)S(1)}, u32[]{:S(2)}, u32[]{:S(2)}) %collective-permute-start.13) | collective-permute-done | bytes 131104 | tf_op jit(solution)/shard_map/ppermute | solution.py:292
  36.9 1.8 %collective-permute-start.15 = (bf16[128,512]{1,0:T(8,128)(2,1)S(1)}, bf16[128,512]{1,0:T(8,128)(2,1)S(1)}, u32[]{:S(2)}, u32[]{:S(2)}) collective-permute-start(bf16[128,512]{1,0:T(8,128)(2,1)S(1)} %get-tuple-element.29.refs_7_), channel_id=1, source_target_pairs={{0,3},{1,2},{2,1},{3,0},{4,7},{5,6},{6,5},{7,4},{8,11},{9,10},{10,... | collective-permute-start | bytes 393224 | tf_op jit(solution)/shard_map/ppermute | solution.py:292
  38.7 1.7 %collective-permute-start = (bf16[128,512]{1,0:T(8,128)(2,1)S(1)}, bf16[128,512]{1,0:T(8,128)(2,1)S(1)}, u32[]{:S(2)}, u32[]{:S(2)}) collective-permute-start(bf16[128,512]{1,0:T(8,128)(2,1)S(1)} %get-tuple-element.24.refs_2_), channel_id=1, source_target_pairs={{0,2},{1,3},{2,0},{3,1},{4,6},{5,7},{6,4},{7,5},{8,10},{9,11},{10,... | collective-permute-start | bytes 393224 | tf_op jit(solution)/shard_map/ppermute | solution.py:292
  41.4 1.8 %collective-permute-start.2 = (bf16[128,512]{1,0:T(8,128)(2,1)S(1)}, bf16[128,512]{1,0:T(8,128)(2,1)S(1)}, u32[]{:S(2)}, u32[]{:S(2)}) collective-permute-start(bf16[128,512]{1,0:T(8,128)(2,1)S(1)} %get-tuple-element.28.refs_6_), channel_id=1, source_target_pairs={{0,3},{1,2},{2,1},{3,0},{4,7},{5,6},{6,5},{7,4},{8,11},{9,10},{10,... | collective-permute-start | bytes 393224 | tf_op jit(solution)/shard_map/ppermute | solution.py:292
  43.8 2.0 %collective-permute-done.14.refs_2_ = bf16[128,512]{1,0:T(8,128)(2,1)S(1)} collective-permute-done((bf16[128,512]{1,0:T(8,128)(2,1)S(1)}, bf16[128,512]{1,0:T(8,128)(2,1)S(1)}, u32[]{:S(2)}, u32[]{:S(2)}) %collective-permute-start.14) | collective-permute-done | bytes 131104 | tf_op jit(solution)/shard_map/ppermute | solution.py:292
  46.3 5.2 %collective-permute-start.17 = (bf16[128,512]{1,0:T(8,128)(2,1)S(1)}, bf16[128,512]{1,0:T(8,128)(2,1)S(1)}, u32[]{:S(2)}, u32[]{:S(2)}) collective-permute-start(bf16[128,512]{1,0:T(8,128)(2,1)S(1)} %shard_map.90.refs_2_), channel_id=1, source_target_pairs={{0,2},{1,3},{2,0},{3,1},{4,6},{5,7},{6,4},{7,5},{8,10},{9,11},{10,... | collective-permute-start | bytes 393224 | tf_op jit(solution)/shard_map/ppermute | solution.py:292
  51.5 7.0 %collective-permute-done.refs_1_ = bf16[128,512]{1,0:T(8,128)(2,1)S(1)} collective-permute-done((bf16[128,512]{1,0:T(8,128)(2,1)S(1)}, bf16[128,512]{1,0:T(8,128)(2,1)S(1)}, u32[]{:S(2)}, u32[]{:S(2)}) %collective-permute-start) | collective-permute-done | bytes 131104 | tf_op jit(solution)/shard_map/ppermute | solution.py:292
  59.0 3.7 %collective-permute-start.16 = (bf16[128,512]{1,0:T(8,128)(2,1)S(1)}, bf16[128,512]{1,0:T(8,128)(2,1)S(1)}, u32[]{:S(2)}, u32[]{:S(2)}) collective-permute-start(bf16[128,512]{1,0:T(8,128)(2,1)S(1)} %shard_map.89.refs_1_), channel_id=1, source_target_pairs={{0,2},{1,3},{2,0},{3,1},{4,6},{5,7},{6,4},{7,5},{8,10},{9,11},{10,... | collective-permute-start | bytes 393224 | tf_op jit(solution)/shard_map/ppermute | solution.py:292
  62.7 2.0 %collective-permute-start.18 = (bf16[128,512]{1,0:T(8,128)(2,1)S(1)}, bf16[128,512]{1,0:T(8,128)(2,1)S(1)}, u32[]{:S(2)}, u32[]{:S(2)}) collective-permute-start(bf16[128,512]{1,0:T(8,128)(2,1)S(1)} %shard_map.89.refs_1_), channel_id=1, source_target_pairs={{0,1},{1,0},{2,3},{3,2},{4,5},{5,4},{6,7},{7,6},{8,9},{9,8},{10,11... | collective-permute-start | bytes 393224 | tf_op jit(solution)/shard_map/ppermute | solution.py:292
  65.7 3.1 %collective-permute-done.16.refs_3_ = bf16[128,512]{1,0:T(8,128)(2,1)S(1)} collective-permute-done((bf16[128,512]{1,0:T(8,128)(2,1)S(1)}, bf16[128,512]{1,0:T(8,128)(2,1)S(1)}, u32[]{:S(2)}, u32[]{:S(2)}) %collective-permute-start.16) | collective-permute-done | bytes 131104 | tf_op jit(solution)/shard_map/ppermute | solution.py:292
  70.4 2.8 %collective-permute-done.18.refs_5_ = bf16[128,512]{1,0:T(8,128)(2,1)S(1)} collective-permute-done((bf16[128,512]{1,0:T(8,128)(2,1)S(1)}, bf16[128,512]{1,0:T(8,128)(2,1)S(1)}, u32[]{:S(2)}, u32[]{:S(2)}) %collective-permute-start.18) | collective-permute-done | bytes 131104 | tf_op jit(solution)/shard_map/ppermute | solution.py:292
  73.2 2.7 %collective-permute-done.21.refs_8_ = bf16[128,512]{1,0:T(8,128)(2,1)S(1)} collective-permute-done((bf16[128,512]{1,0:T(8,128)(2,1)S(1)}, bf16[128,512]{1,0:T(8,128)(2,1)S(1)}, u32[]{:S(2)}, u32[]{:S(2)}) %collective-permute-start.21) | collective-permute-done | bytes 131104 | tf_op jit(solution)/shard_map/ppermute | solution.py:292
  83.8 2.4 %collective-permute-done.24 = f32[64,512]{1,0:T(8,128)S(1)} collective-permute-done((f32[64,512]{1,0:T(8,128)S(1)}, f32[64,512]{1,0:T(8,128)S(1)}, u32[]{:S(2)}, u32[]{:S(2)}) %collective-permute-start.24) | collective-permute-done | bytes 131104 | tf_op jit(solution)/shard_map/ppermute | solution.py:295
  86.3 3.2 %collective-permute-done.26 = f32[64,512]{1,0:T(8,128)S(1)} collective-permute-done((f32[64,512]{1,0:T(8,128)S(1)}, f32[64,512]{1,0:T(8,128)S(1)}, u32[]{:S(2)}, u32[]{:S(2)}) %collective-permute-start.26) | collective-permute-done | bytes 131104 | tf_op jit(solution)/shard_map/ppermute | solution.py:295
  93.1 2.5 %collective-permute-done.30.refs_2_.refs_3_ = f32[64,512]{1,0:T(8,128)S(1)} collective-permute-done((f32[64,512]{1,0:T(8,128)S(1)}, f32[64,512]{1,0:T(8,128)S(1)}, u32[]{:S(2)}, u32[]{:S(2)}) %collective-permute-start.30) | collective-permute-done | bytes 131104 | tf_op jit(solution)/shard_map/ppermute | solution.py:295
  95.6 2.4 %collective-permute-done.32.refs_4_.refs_5_ = f32[64,512]{1,0:T(8,128)S(1)} collective-permute-done((f32[64,512]{1,0:T(8,128)S(1)}, f32[64,512]{1,0:T(8,128)S(1)}, u32[]{:S(2)}, u32[]{:S(2)}) %collective-permute-start.32) | collective-permute-done | bytes 131104 | tf_op jit(solution)/shard_map/ppermute | solution.py:295
  99.5 1.7 %shard_map.96 = (f32[2,64,512]{2,1,0:T(8,128)S(1)}, f32[2,64,512]{2,1,0:T(8,128)S(1)}) custom-call(s32[51]{0:T(128)S(1)} %concatenate.3.where, f32[256,512]{1,0:T(8,128)S(1)} %shard_map.95.refs_0_, f32[64,512]{1,0:T(8,128)S(1)} %add_add_fusion.refs_0_.refs_1_, f32[64,512]{1,0:T(8,128)S(1)} %collective-permute-done.29.refs_1_.refs_2_, ...), custom_call_target="tpu_custom_call" | custom-call | tf_op jit(solution)/shard_map/pallas_call | solution.py:263
  101.3 8.5 %collective-permute-done.45 = f32[2,64,512]{2,1,0:T(8,128)S(1)} collective-permute-done((f32[2,64,512]{2,1,0:T(8,128)S(1)}, f32[2,64,512]{2,1,0:T(8,128)S(1)}, u32[]{:S(2)}, u32[]{:S(2)}) %collective-permute-start.45) | collective-permute-done | bytes 262176 | tf_op jit(solution)/shard_map/ppermute | solution.py:292
  110.9 1.9 %shard_map.92 = f32[32,640]{1,0:T(8,128)S(1)} custom-call(s32[51]{0:T(128)S(1)} %concatenate.3.where, f32[64,512]{1,0:T(8,128)S(1)} %add_add_fusion.refs_0_.refs_1_, f32[64,512]{1,0:T(8,128)S(1)} %collective-permute-done.29.refs_1_.refs_2_, f32[64,512]{1,0:T(8,128)S(1)} %collective-permute-done.30.refs_2_.refs_3_, ...), custom_call_target="tpu_custom_call" | custom-call | tf_op jit(solution)/shard_map/pallas_call | solution.py:263
  114.3 9.9 %collective-permute-done.46 = f32[2,64,512]{2,1,0:T(8,128)S(1)} collective-permute-done((f32[2,64,512]{2,1,0:T(8,128)S(1)}, f32[2,64,512]{2,1,0:T(8,128)S(1)}, u32[]{:S(2)}, u32[]{:S(2)}) %collective-permute-start.46) | collective-permute-done | bytes 262176 | tf_op jit(solution)/shard_map/ppermute | solution.py:292
  124.3 2.2 %collective-permute-start.37 = (f32[32,640]{1,0:T(8,128)S(1)}, f32[32,640]{1,0:T(8,128)S(1)}, u32[]{:S(2)}, u32[]{:S(2)}) collective-permute-start(f32[32,640]{1,0:T(8,128)S(1)} %add.44), channel_id=1, source_target_pairs={{0,2},{1,3},{2,0},{3,1},{4,6},{5,7},{6,4},{7,5},{8,10},{9,11},{10,... | collective-permute-start | bytes 245768 | tf_op jit(solution)/shard_map/ppermute | solution.py:292
  126.5 5.5 %collective-permute-done.37 = f32[32,640]{1,0:T(8,128)S(1)} collective-permute-done((f32[32,640]{1,0:T(8,128)S(1)}, f32[32,640]{1,0:T(8,128)S(1)}, u32[]{:S(2)}, u32[]{:S(2)}) %collective-permute-start.37) | collective-permute-done | bytes 81952 | tf_op jit(solution)/shard_map/ppermute | solution.py:292
  132.6 1.7 %collective-permute-start.41 = (f32[32,640]{1,0:T(8,128)S(1)}, f32[32,640]{1,0:T(8,128)S(1)}, u32[]{:S(2)}, u32[]{:S(2)}) collective-permute-start(f32[32,640]{1,0:T(8,128)S(1)} %add.45.refs_0_), channel_id=1, source_target_pairs={{0,16},{4,20},{8,24},{12,28},{16,0},{20,4},{24,8},{28,12},{1,17},{... | collective-permute-start | bytes 245768 | tf_op jit(solution)/shard_map/ppermute | solution.py:295
  135.6 1.7 %collective-permute-done.39.refs_2_ = f32[32,640]{1,0:T(8,128)S(1)} collective-permute-done((f32[32,640]{1,0:T(8,128)S(1)}, f32[32,640]{1,0:T(8,128)S(1)}, u32[]{:S(2)}, u32[]{:S(2)}) %collective-permute-start.39) | collective-permute-done | bytes 81952 | tf_op jit(solution)/shard_map/ppermute | solution.py:295
  137.8 1.8 %collective-permute-done.43.refs_6_ = f32[32,640]{1,0:T(8,128)S(1)} collective-permute-done((f32[32,640]{1,0:T(8,128)S(1)}, f32[32,640]{1,0:T(8,128)S(1)}, u32[]{:S(2)}, u32[]{:S(2)}) %collective-permute-start.43) | collective-permute-done | bytes 81952 | tf_op jit(solution)/shard_map/ppermute | solution.py:295
  141.0 7.6 %shard_map.93.begun = f32[512,512]{1,0:T(8,128)S(1)} custom-call(s32[51]{0:T(128)S(1)} %concatenate.3.where, f32[32,640]{1,0:T(8,128)S(1)} %add.45.refs_0_, f32[32,640]{1,0:T(8,128)S(1)} %collective-permute-done.38.refs_1_, f32[32,640]{1,0:T(8,128)S(1)} %collective-permute-done.39.refs_2_, f32[32,640]{1,0:T(8,128)S(1)} %collective-permute-done.40.refs_3_, ...), custom_call_target="tpu_custom_call" | custom-call | tf_op jit(solution)/shard_map/pallas_call | solution.py:263
  148.6 8.5 %shard_map.94.refs_0_ = f32[512,512]{1,0:T(8,128)S(1)} custom-call(f32[512,512]{1,0:T(8,128)S(1)} %shard_map.93.begun), custom_call_target="tpu_custom_call" | custom-call | tf_op jit(solution)/shard_map/pallas_call | solution.py:263
  157.1 2.7 %shard_map.97 = (f32[64,512]{1,0:T(8,128)}, f32[256,512]{1,0:T(8,128)}) custom-call(s32[51]{0:T(128)S(1)} %concatenate.3.where, f32[512,512]{1,0:T(8,128)S(1)} %shard_map.94.refs_0_, f32[64,512]{1,0:T(8,128)S(1)} %add_add_fusion.refs_0_.refs_1_, f32[2,64,512]{2,1,0:T(8,128)S(1)} %add.47.refs_2_, f32[2,64,512]{2,1,0:T(8,128)S(1)} %collective-permute-done.47.refs_3_), custom_call_target="tpu_custom_call" | custom-call | tf_op jit(solution)/shard_map/pallas_call | solution.py:263
  (98 shorter events, 38.0 us)
Async XLA Ops:
  1.5 7.1 %collective-permute-start.3 = (bf16[64,512]{1,0:T(8,128)(2,1)S(1)}, bf16[64,512]{1,0:T(8,128)(2,1)S(1)}, u32[]{:S(2)}, u32[]{:S(2)}) collective-permute-start(bf16[64,512]{1,0:T(8,128)(2,1)S(1)} %constant_dynamic-slice_fusion), channel_id=1, source_target_pairs={{0,2},{1,3},{2,0},{3,1},{4,6},{5,7},{6,4},{7,5},{8,10},{9,11},{10,... | collective-permute-start | bytes 196616 | tf_op jit(solution)/shard_map/ppermute | solution.py:292
  7.1 6.1 %collective-permute-start.5 = (bf16[64,512]{1,0:T(8,128)(2,1)S(1)}, bf16[64,512]{1,0:T(8,128)(2,1)S(1)}, u32[]{:S(2)}, u32[]{:S(2)}) collective-permute-start(bf16[64,512]{1,0:T(8,128)(2,1)S(1)} %constant_dynamic-slice_fusion), channel_id=1, source_target_pairs={{0,3},{1,2},{2,1},{3,0},{4,7},{5,6},{6,5},{7,4},{8,11},{9,10},{10,... | collective-permute-start | bytes 196616 | tf_op jit(solution)/shard_map/ppermute | solution.py:292
  13.2 8.4 %collective-permute-start.9 = (bf16[3,64,512]{2,1,0:T(8,128)(2,1)S(1)}, bf16[3,64,512]{2,1,0:T(8,128)(2,1)S(1)}, u32[]{:S(2)}, u32[]{:S(2)}) collective-permute-start(bf16[3,64,512]{2,1,0:T(8,128)(2,1)S(1)} %pad_maximum_fusion.refs_0_), channel_id=1, source_target_pairs={{0,16},{4,20},{8,24},{12,28},{16,0},{20,4},{24,8},{28,12},{1,17},{... | collective-permute-start | bytes 589832 | tf_op jit(solution)/shard_map/ppermute | solution.py:295
  14.8 7.8 %collective-permute-start.11 = (bf16[3,64,512]{2,1,0:T(8,128)(2,1)S(1)}, bf16[3,64,512]{2,1,0:T(8,128)(2,1)S(1)}, u32[]{:S(2)}, u32[]{:S(2)}) collective-permute-start(bf16[3,64,512]{2,1,0:T(8,128)(2,1)S(1)} %pad_maximum_fusion.refs_0_), channel_id=1, source_target_pairs={{0,24},{4,28},{8,16},{12,20},{16,8},{20,12},{24,0},{28,4},{1,25},{... | collective-permute-start | bytes 589832 | tf_op jit(solution)/shard_map/ppermute | solution.py:295
  16.2 7.5 %collective-permute-start.7 = (bf16[3,64,512]{2,1,0:T(8,128)(2,1)S(1)}, bf16[3,64,512]{2,1,0:T(8,128)(2,1)S(1)}, u32[]{:S(2)}, u32[]{:S(2)}) collective-permute-start(bf16[3,64,512]{2,1,0:T(8,128)(2,1)S(1)} %pad_maximum_fusion.refs_0_), channel_id=1, source_target_pairs={{0,8},{4,12},{8,0},{12,4},{16,24},{20,28},{24,16},{28,20},{1,9},{5... | collective-permute-start | bytes 589832 | tf_op jit(solution)/shard_map/ppermute | solution.py:295
  16.8 20.2 %collective-permute-start.6 = (bf16[3,64,512]{2,1,0:T(8,128)(2,1)S(1)}, bf16[3,64,512]{2,1,0:T(8,128)(2,1)S(1)}, u32[]{:S(2)}, u32[]{:S(2)}) collective-permute-start(bf16[3,64,512]{2,1,0:T(8,128)(2,1)S(1)} %pad_maximum_fusion.refs_0_), channel_id=1, source_target_pairs={{0,4},{4,0},{8,12},{12,8},{16,20},{20,16},{24,28},{28,24},{1,5},{5... | collective-permute-start | bytes 589832 | tf_op jit(solution)/shard_map/ppermute | solution.py:295
  21.6 17.1 %collective-permute-start.10 = (bf16[3,64,512]{2,1,0:T(8,128)(2,1)S(1)}, bf16[3,64,512]{2,1,0:T(8,128)(2,1)S(1)}, u32[]{:S(2)}, u32[]{:S(2)}) collective-permute-start(bf16[3,64,512]{2,1,0:T(8,128)(2,1)S(1)} %collective-permute-done.9.refs_4_), channel_id=1, source_target_pairs={{0,4},{4,0},{8,12},{12,8},{16,20},{20,16},{24,28},{28,24},{1,5},{5... | collective-permute-start | bytes 589832 | tf_op jit(solution)/shard_map/ppermute | solution.py:295
  22.6 17.9 %collective-permute-start.12 = (bf16[3,64,512]{2,1,0:T(8,128)(2,1)S(1)}, bf16[3,64,512]{2,1,0:T(8,128)(2,1)S(1)}, u32[]{:S(2)}, u32[]{:S(2)}) collective-permute-start(bf16[3,64,512]{2,1,0:T(8,128)(2,1)S(1)} %collective-permute-done.11.refs_6_), channel_id=1, source_target_pairs={{0,4},{4,0},{8,12},{12,8},{16,20},{20,16},{24,28},{28,24},{1,5},{5... | collective-permute-start | bytes 589832 | tf_op jit(solution)/shard_map/ppermute | solution.py:295
  23.8 17.6 %collective-permute-start.8 = (bf16[3,64,512]{2,1,0:T(8,128)(2,1)S(1)}, bf16[3,64,512]{2,1,0:T(8,128)(2,1)S(1)}, u32[]{:S(2)}, u32[]{:S(2)}) collective-permute-start(bf16[3,64,512]{2,1,0:T(8,128)(2,1)S(1)} %collective-permute-done.7.refs_2_), channel_id=1, source_target_pairs={{0,4},{4,0},{8,12},{12,8},{16,20},{20,16},{24,28},{28,24},{1,5},{5... | collective-permute-start | bytes 589832 | tf_op jit(solution)/shard_map/ppermute | solution.py:295
  27.3 9.7 %collective-permute-start.13 = (bf16[128,512]{1,0:T(8,128)(2,1)S(1)}, bf16[128,512]{1,0:T(8,128)(2,1)S(1)}, u32[]{:S(2)}, u32[]{:S(2)}) collective-permute-start(bf16[128,512]{1,0:T(8,128)(2,1)S(1)} %get-tuple-element.25.refs_3_), channel_id=1, source_target_pairs={{0,2},{1,3},{2,0},{3,1},{4,6},{5,7},{6,4},{7,5},{8,10},{9,11},{10,... | collective-permute-start | bytes 393224 | tf_op jit(solution)/shard_map/ppermute | solution.py:292
  36.9 8.9 %collective-permute-start.14 = (bf16[128,512]{1,0:T(8,128)(2,1)S(1)}, bf16[128,512]{1,0:T(8,128)(2,1)S(1)}, u32[]{:S(2)}, u32[]{:S(2)}) collective-permute-start(bf16[128,512]{1,0:T(8,128)(2,1)S(1)} %get-tuple-element.27.refs_5_), channel_id=1, source_target_pairs={{0,1},{1,0},{2,3},{3,2},{4,5},{5,4},{6,7},{7,6},{8,9},{9,8},{10,11... | collective-permute-start | bytes 393224 | tf_op jit(solution)/shard_map/ppermute | solution.py:292
  36.9 8.9 %collective-permute-start.15 = (bf16[128,512]{1,0:T(8,128)(2,1)S(1)}, bf16[128,512]{1,0:T(8,128)(2,1)S(1)}, u32[]{:S(2)}, u32[]{:S(2)}) collective-permute-start(bf16[128,512]{1,0:T(8,128)(2,1)S(1)} %get-tuple-element.29.refs_7_), channel_id=1, source_target_pairs={{0,3},{1,2},{2,1},{3,0},{4,7},{5,6},{6,5},{7,4},{8,11},{9,10},{10,... | collective-permute-start | bytes 393224 | tf_op jit(solution)/shard_map/ppermute | solution.py:292
  38.7 19.8 %collective-permute-start = (bf16[128,512]{1,0:T(8,128)(2,1)S(1)}, bf16[128,512]{1,0:T(8,128)(2,1)S(1)}, u32[]{:S(2)}, u32[]{:S(2)}) collective-permute-start(bf16[128,512]{1,0:T(8,128)(2,1)S(1)} %get-tuple-element.24.refs_2_), channel_id=1, source_target_pairs={{0,2},{1,3},{2,0},{3,1},{4,6},{5,7},{6,4},{7,5},{8,10},{9,11},{10,... | collective-permute-start | bytes 393224 | tf_op jit(solution)/shard_map/ppermute | solution.py:292
  40.4 18.1 %collective-permute-start.1 = (bf16[128,512]{1,0:T(8,128)(2,1)S(1)}, bf16[128,512]{1,0:T(8,128)(2,1)S(1)}, u32[]{:S(2)}, u32[]{:S(2)}) collective-permute-start(bf16[128,512]{1,0:T(8,128)(2,1)S(1)} %get-tuple-element.26.refs_4_), channel_id=1, source_target_pairs={{0,1},{1,0},{2,3},{3,2},{4,5},{5,4},{6,7},{7,6},{8,9},{9,8},{10,11... | collective-permute-start | bytes 393224 | tf_op jit(solution)/shard_map/ppermute | solution.py:292
  41.4 17.2 %collective-permute-start.2 = (bf16[128,512]{1,0:T(8,128)(2,1)S(1)}, bf16[128,512]{1,0:T(8,128)(2,1)S(1)}, u32[]{:S(2)}, u32[]{:S(2)}) collective-permute-start(bf16[128,512]{1,0:T(8,128)(2,1)S(1)} %get-tuple-element.28.refs_6_), channel_id=1, source_target_pairs={{0,3},{1,2},{2,1},{3,0},{4,7},{5,6},{6,5},{7,4},{8,11},{9,10},{10,... | collective-permute-start | bytes 393224 | tf_op jit(solution)/shard_map/ppermute | solution.py:292
  46.3 19.4 %collective-permute-start.17 = (bf16[128,512]{1,0:T(8,128)(2,1)S(1)}, bf16[128,512]{1,0:T(8,128)(2,1)S(1)}, u32[]{:S(2)}, u32[]{:S(2)}) collective-permute-start(bf16[128,512]{1,0:T(8,128)(2,1)S(1)} %shard_map.90.refs_2_), channel_id=1, source_target_pairs={{0,2},{1,3},{2,0},{3,1},{4,6},{5,7},{6,4},{7,5},{8,10},{9,11},{10,... | collective-permute-start | bytes 393224 | tf_op jit(solution)/shard_map/ppermute | solution.py:292
  59.0 9.7 %collective-permute-start.16 = (bf16[128,512]{1,0:T(8,128)(2,1)S(1)}, bf16[128,512]{1,0:T(8,128)(2,1)S(1)}, u32[]{:S(2)}, u32[]{:S(2)}) collective-permute-start(bf16[128,512]{1,0:T(8,128)(2,1)S(1)} %shard_map.89.refs_1_), channel_id=1, source_target_pairs={{0,2},{1,3},{2,0},{3,1},{4,6},{5,7},{6,4},{7,5},{8,10},{9,11},{10,... | collective-permute-start | bytes 393224 | tf_op jit(solution)/shard_map/ppermute | solution.py:292
  62.7 7.7 %collective-permute-start.19 = (bf16[128,512]{1,0:T(8,128)(2,1)S(1)}, bf16[128,512]{1,0:T(8,128)(2,1)S(1)}, u32[]{:S(2)}, u32[]{:S(2)}) collective-permute-start(bf16[128,512]{1,0:T(8,128)(2,1)S(1)} %shard_map.90.refs_2_), channel_id=1, source_target_pairs={{0,1},{1,0},{2,3},{3,2},{4,5},{5,4},{6,7},{7,6},{8,9},{9,8},{10,11... | collective-permute-start | bytes 393224 | tf_op jit(solution)/shard_map/ppermute | solution.py:292
  62.7 10.5 %collective-permute-start.18 = (bf16[128,512]{1,0:T(8,128)(2,1)S(1)}, bf16[128,512]{1,0:T(8,128)(2,1)S(1)}, u32[]{:S(2)}, u32[]{:S(2)}) collective-permute-start(bf16[128,512]{1,0:T(8,128)(2,1)S(1)} %shard_map.89.refs_1_), channel_id=1, source_target_pairs={{0,1},{1,0},{2,3},{3,2},{4,5},{5,4},{6,7},{7,6},{8,9},{9,8},{10,11... | collective-permute-start | bytes 393224 | tf_op jit(solution)/shard_map/ppermute | solution.py:292
  65.7 10.2 %collective-permute-start.21 = (bf16[128,512]{1,0:T(8,128)(2,1)S(1)}, bf16[128,512]{1,0:T(8,128)(2,1)S(1)}, u32[]{:S(2)}, u32[]{:S(2)}) collective-permute-start(bf16[128,512]{1,0:T(8,128)(2,1)S(1)} %collective-permute-done.17.refs_4_), channel_id=1, source_target_pairs={{0,1},{1,0},{2,3},{3,2},{4,5},{5,4},{6,7},{7,6},{8,9},{9,8},{10,11... | collective-permute-start | bytes 393224 | tf_op jit(solution)/shard_map/ppermute | solution.py:292
  68.7 8.6 %collective-permute-start.20 = (bf16[128,512]{1,0:T(8,128)(2,1)S(1)}, bf16[128,512]{1,0:T(8,128)(2,1)S(1)}, u32[]{:S(2)}, u32[]{:S(2)}) collective-permute-start(bf16[128,512]{1,0:T(8,128)(2,1)S(1)} %collective-permute-done.16.refs_3_), channel_id=1, source_target_pairs={{0,1},{1,0},{2,3},{3,2},{4,5},{5,4},{6,7},{7,6},{8,9},{9,8},{10,11... | collective-permute-start | bytes 393224 | tf_op jit(solution)/shard_map/ppermute | solution.py:292
  80.1 6.2 %collective-permute-start.24 = (f32[64,512]{1,0:T(8,128)S(1)}, f32[64,512]{1,0:T(8,128)S(1)}, u32[]{:S(2)}, u32[]{:S(2)}) collective-permute-start(f32[64,512]{1,0:T(8,128)S(1)} %add.38), channel_id=1, source_target_pairs={{0,8},{4,12},{8,0},{12,4},{16,24},{20,28},{24,16},{28,20},{1,9},{5... | collective-permute-start | bytes 393224 | tf_op jit(solution)/shard_map/ppermute | solution.py:295
  81.3 8.1 %collective-permute-start.26 = (f32[64,512]{1,0:T(8,128)S(1)}, f32[64,512]{1,0:T(8,128)S(1)}, u32[]{:S(2)}, u32[]{:S(2)}) collective-permute-start(f32[64,512]{1,0:T(8,128)S(1)} %add.40), channel_id=1, source_target_pairs={{0,16},{4,20},{8,24},{12,28},{16,0},{20,4},{24,8},{28,12},{1,17},{... | collective-permute-start | bytes 393224 | tf_op jit(solution)/shard_map/ppermute | solution.py:295
  83.0 6.5 %collective-permute-start.28 = (f32[64,512]{1,0:T(8,128)S(1)}, f32[64,512]{1,0:T(8,128)S(1)}, u32[]{:S(2)}, u32[]{:S(2)}) collective-permute-start(f32[64,512]{1,0:T(8,128)S(1)} %add.42), channel_id=1, source_target_pairs={{0,24},{4,28},{8,16},{12,20},{16,8},{20,12},{24,0},{28,4},{1,25},{... | collective-permute-start | bytes 393224 | tf_op jit(solution)/shard_map/ppermute | solution.py:295
  90.8 7.2 %collective-permute-start.32 = (f32[64,512]{1,0:T(8,128)S(1)}, f32[64,512]{1,0:T(8,128)S(1)}, u32[]{:S(2)}, u32[]{:S(2)}) collective-permute-start(f32[64,512]{1,0:T(8,128)S(1)} %add_add_fusion.refs_0_.refs_1_), channel_id=1, source_target_pairs={{0,16},{4,20},{8,24},{12,28},{16,0},{20,4},{24,8},{28,12},{1,17},{... | collective-permute-start | bytes 393224 | tf_op jit(solution)/shard_map/ppermute | solution.py:295
  91.8 6.2 %collective-permute-start.34 = (f32[64,512]{1,0:T(8,128)S(1)}, f32[64,512]{1,0:T(8,128)S(1)}, u32[]{:S(2)}, u32[]{:S(2)}) collective-permute-start(f32[64,512]{1,0:T(8,128)S(1)} %add_add_fusion.refs_0_.refs_1_), channel_id=1, source_target_pairs={{0,24},{4,28},{8,16},{12,20},{16,8},{20,12},{24,0},{28,4},{1,25},{... | collective-permute-start | bytes 393224 | tf_op jit(solution)/shard_map/ppermute | solution.py:295
  93.1 6.3 %collective-permute-start.29 = (f32[64,512]{1,0:T(8,128)S(1)}, f32[64,512]{1,0:T(8,128)S(1)}, u32[]{:S(2)}, u32[]{:S(2)}) collective-permute-start(f32[64,512]{1,0:T(8,128)S(1)} %add_add_fusion.refs_0_.refs_1_), channel_id=1, source_target_pairs={{0,4},{4,0},{8,12},{12,8},{16,20},{20,16},{24,28},{28,24},{1,5},{5... | collective-permute-start | bytes 393224 | tf_op jit(solution)/shard_map/ppermute | solution.py:295
  101.2 8.6 %collective-permute-start.45 = (f32[2,64,512]{2,1,0:T(8,128)S(1)}, f32[2,64,512]{2,1,0:T(8,128)S(1)}, u32[]{:S(2)}, u32[]{:S(2)}) collective-permute-start(f32[2,64,512]{2,1,0:T(8,128)S(1)} %get-tuple-element.39), channel_id=1, source_target_pairs={{0,1},{1,0},{2,3},{3,2},{4,5},{5,4},{6,7},{7,6},{8,9},{9,8},{10,11... | collective-permute-start | bytes 786440 | tf_op jit(solution)/shard_map/ppermute | solution.py:292
  109.9 14.3 %collective-permute-start.46 = (f32[2,64,512]{2,1,0:T(8,128)S(1)}, f32[2,64,512]{2,1,0:T(8,128)S(1)}, u32[]{:S(2)}, u32[]{:S(2)}) collective-permute-start(f32[2,64,512]{2,1,0:T(8,128)S(1)} %rev.3), channel_id=1, source_target_pairs={{0,2},{1,3},{2,0},{3,1},{4,6},{5,7},{6,4},{7,5},{8,10},{9,11},{10,... | collective-permute-start | bytes 786440 | tf_op jit(solution)/shard_map/ppermute | solution.py:292
  112.7 11.5 %collective-permute-start.36 = (f32[32,640]{1,0:T(8,128)S(1)}, f32[32,640]{1,0:T(8,128)S(1)}, u32[]{:S(2)}, u32[]{:S(2)}) collective-permute-start(f32[32,640]{1,0:T(8,128)S(1)} %shard_map.92), channel_id=1, source_target_pairs={{0,1},{1,0},{2,3},{3,2},{4,5},{5,4},{6,7},{7,6},{8,9},{9,8},{10,11... | collective-permute-start | bytes 245768 | tf_op jit(solution)/shard_map/ppermute | solution.py:292
  124.2 32.9 %collective-permute-start.47 = (f32[2,64,512]{2,1,0:T(8,128)S(1)}, f32[2,64,512]{2,1,0:T(8,128)S(1)}, u32[]{:S(2)}, u32[]{:S(2)}) collective-permute-start(f32[2,64,512]{2,1,0:T(8,128)S(1)} %add.47.refs_2_), channel_id=1, source_target_pairs={{0,1},{1,0},{2,3},{3,2},{4,5},{5,4},{6,7},{7,6},{8,9},{9,8},{10,11... | collective-permute-start | bytes 786440 | tf_op jit(solution)/shard_map/ppermute | solution.py:292
  124.3 7.7 %collective-permute-start.37 = (f32[32,640]{1,0:T(8,128)S(1)}, f32[32,640]{1,0:T(8,128)S(1)}, u32[]{:S(2)}, u32[]{:S(2)}) collective-permute-start(f32[32,640]{1,0:T(8,128)S(1)} %add.44), channel_id=1, source_target_pairs={{0,2},{1,3},{2,0},{3,1},{4,6},{5,7},{6,4},{7,5},{8,10},{9,11},{10,... | collective-permute-start | bytes 245768 | tf_op jit(solution)/shard_map/ppermute | solution.py:292
  (20 other events, 108.6 us)

commit v2 on v1

--- a/solution.py
+++ b/solution.py
@@ -317,10 +317,10 @@
         [tile_values[0, 0]],
     )
     own_terms = lax.dynamic_slice_in_dim(sketch, doc * share, share, 0)
-    blocks = [
-        [dense[h]] + [along(dense[i * HALVES + h], v_places[i]) for i in range(1, n_vocab)]
-        for h in range(HALVES)
-    ]
+    blocks = []
+    for h in range(HALVES):
+        moved = [along(dense[i * HALVES + h], v_places[i]) for i in range(1, n_vocab)]
+        blocks.append([dense[h]] + moved)
     others = jnp.stack([along(own_terms, place) for place in v_places[1:]])
     term_pieces = spread(others)
     other_sketch = call(

time: 160 us -> 160 us (level)
  no operation moved by 1% of the time
where the time goes in v2:
time: 160 us
  waiting for transfers between devices  80.3 us (50%)
  starting transfers between devices  47.6 us (30%)
  Pallas kernels  27.1 us (17%)
  local copies, waits for them, and re-layouts  2.94 us (2%)
    ppermute x20, waiting for transfers between devices, along(): return lax.ppermute(x, 'vocab', [(a, a ^ place) for a in range(n_vocab)])  57.4 us
    ppermute x20, starting transfers between devices, along(): return lax.ppermute(x, 'vocab', [(a, a ^ place) for a in range(n_vocab)])  31.3 us
    pallas_call x12, Pallas kernels, call(): pl.pallas_call(kernel, out_shape=outs, in_specs=[smem] * len(scalars) + [...  27.1 us
    ppermute x28, waiting for transfers between devices, across(): return lax.ppermute(x, 'doc', [(a, a ^ place) for a in range(n_doc)])  23 us
    ppermute x28, starting transfers between devices, across(): return lax.ppermute(x, 'doc', [(a, a ^ place) for a in range(n_doc)])  16.4 us
  transfers between devices with their start and end apart: 48, of which 28 were waited for; matrix products, arithmetic and copies ran while one was open for 1% of the time, Pallas kernels for 13%

profile of v2, /device:TPU:0, one launch (start us, length us, event | category | flops | bytes accessed | tf_op | source)
XLA Modules:
  0.0 159.8 jit_solution(15723834172524078520)
XLA Ops:
  1.5 4.1 %collective-permute-start.3 = (bf16[64,512]{1,0:T(8,128)(2,1)S(1)}, bf16[64,512]{1,0:T(8,128)(2,1)S(1)}, u32[]{:S(2)}, u32[]{:S(2)}) collective-permute-start(bf16[64,512]{1,0:T(8,128)(2,1)S(1)} %constant_dynamic-slice_fusion), channel_id=1, source_target_pairs={{0,2},{1,3},{2,0},{3,1},{4,6},{5,7},{6,4},{7,5},{8,10},{9,11},{10,... | collective-permute-start | bytes 196616 | tf_op jit(solution)/shard_map/ppermute | solution.py:292
  9.8 3.4 %collective-permute-done.5 = bf16[64,512]{1,0:T(8,128)(2,1)S(1)} collective-permute-done((bf16[64,512]{1,0:T(8,128)(2,1)S(1)}, bf16[64,512]{1,0:T(8,128)(2,1)S(1)}, u32[]{:S(2)}, u32[]{:S(2)}) %collective-permute-start.5) | collective-permute-done | bytes 65568 | tf_op jit(solution)/shard_map/ppermute | solution.py:292
  16.8 4.9 %collective-permute-done.9.refs_4_ = bf16[3,64,512]{2,1,0:T(8,128)(2,1)S(1)} collective-permute-done((bf16[3,64,512]{2,1,0:T(8,128)(2,1)S(1)}, bf16[3,64,512]{2,1,0:T(8,128)(2,1)S(1)}, u32[]{:S(2)}, u32[]{:S(2)}) %collective-permute-start.9) | collective-permute-done | bytes 196640 | tf_op jit(solution)/shard_map/ppermute | solution.py:295
  27.3 2.6 %collective-permute-start.13 = (bf16[128,512]{1,0:T(8,128)(2,1)S(1)}, bf16[128,512]{1,0:T(8,128)(2,1)S(1)}, u32[]{:S(2)}, u32[]{:S(2)}) collective-permute-start(bf16[128,512]{1,0:T(8,128)(2,1)S(1)} %get-tuple-element.25.refs_3_), channel_id=1, source_target_pairs={{0,2},{1,3},{2,0},{3,1},{4,6},{5,7},{6,4},{7,5},{8,10},{9,11},{10,... | collective-permute-start | bytes 393224 | tf_op jit(solution)/shard_map/ppermute | solution.py:292
  29.9 7.0 %collective-permute-done.13.refs_1_ = bf16[128,512]{1,0:T(8,128)(2,1)S(1)} collective-permute-done((bf16[128,512]{1,0:T(8,128)(2,1)S(1)}, bf16[128,512]{1,0:T(8,128)(2,1)S(1)}, u32[]{:S(2)}, u32[]{:S(2)}) %collective-permute-start.13) | collective-permute-done | bytes 131104 | tf_op jit(solution)/shard_map/ppermute | solution.py:292
  36.9 1.8 %collective-permute-start.15 = (bf16[128,512]{1,0:T(8,128)(2,1)S(1)}, bf16[128,512]{1,0:T(8,128)(2,1)S(1)}, u32[]{:S(2)}, u32[]{:S(2)}) collective-permute-start(bf16[128,512]{1,0:T(8,128)(2,1)S(1)} %get-tuple-element.29.refs_7_), channel_id=1, source_target_pairs={{0,3},{1,2},{2,1},{3,0},{4,7},{5,6},{6,5},{7,4},{8,11},{9,10},{10,... | collective-permute-start | bytes 393224 | tf_op jit(solution)/shard_map/ppermute | solution.py:292
  38.7 1.7 %collective-permute-start = (bf16[128,512]{1,0:T(8,128)(2,1)S(1)}, bf16[128,512]{1,0:T(8,128)(2,1)S(1)}, u32[]{:S(2)}, u32[]{:S(2)}) collective-permute-start(bf16[128,512]{1,0:T(8,128)(2,1)S(1)} %get-tuple-element.24.refs_2_), channel_id=1, source_target_pairs={{0,2},{1,3},{2,0},{3,1},{4,6},{5,7},{6,4},{7,5},{8,10},{9,11},{10,... | collective-permute-start | bytes 393224 | tf_op jit(solution)/shard_map/ppermute | solution.py:292
  41.4 1.8 %collective-permute-start.2 = (bf16[128,512]{1,0:T(8,128)(2,1)S(1)}, bf16[128,512]{1,0:T(8,128)(2,1)S(1)}, u32[]{:S(2)}, u32[]{:S(2)}) collective-permute-start(bf16[128,512]{1,0:T(8,128)(2,1)S(1)} %get-tuple-element.28.refs_6_), channel_id=1, source_target_pairs={{0,3},{1,2},{2,1},{3,0},{4,7},{5,6},{6,5},{7,4},{8,11},{9,10},{10,... | collective-permute-start | bytes 393224 | tf_op jit(solution)/shard_map/ppermute | solution.py:292
  43.8 2.0 %collective-permute-done.14.refs_2_ = bf16[128,512]{1,0:T(8,128)(2,1)S(1)} collective-permute-done((bf16[128,512]{1,0:T(8,128)(2,1)S(1)}, bf16[128,512]{1,0:T(8,128)(2,1)S(1)}, u32[]{:S(2)}, u32[]{:S(2)}) %collective-permute-start.14) | collective-permute-done | bytes 131104 | tf_op jit(solution)/shard_map/ppermute | solution.py:292
  46.3 5.2 %collective-permute-start.17 = (bf16[128,512]{1,0:T(8,128)(2,1)S(1)}, bf16[128,512]{1,0:T(8,128)(2,1)S(1)}, u32[]{:S(2)}, u32[]{:S(2)}) collective-permute-start(bf16[128,512]{1,0:T(8,128)(2,1)S(1)} %shard_map.90.refs_2_), channel_id=1, source_target_pairs={{0,2},{1,3},{2,0},{3,1},{4,6},{5,7},{6,4},{7,5},{8,10},{9,11},{10,... | collective-permute-start | bytes 393224 | tf_op jit(solution)/shard_map/ppermute | solution.py:292
  51.5 7.0 %collective-permute-done.refs_1_ = bf16[128,512]{1,0:T(8,128)(2,1)S(1)} collective-permute-done((bf16[128,512]{1,0:T(8,128)(2,1)S(1)}, bf16[128,512]{1,0:T(8,128)(2,1)S(1)}, u32[]{:S(2)}, u32[]{:S(2)}) %collective-permute-start) | collective-permute-done | bytes 131104 | tf_op jit(solution)/shard_map/ppermute | solution.py:292
  59.0 3.7 %collective-permute-start.16 = (bf16[128,512]{1,0:T(8,128)(2,1)S(1)}, bf16[128,512]{1,0:T(8,128)(2,1)S(1)}, u32[]{:S(2)}, u32[]{:S(2)}) collective-permute-start(bf16[128,512]{1,0:T(8,128)(2,1)S(1)} %shard_map.89.refs_1_), channel_id=1, source_target_pairs={{0,2},{1,3},{2,0},{3,1},{4,6},{5,7},{6,4},{7,5},{8,10},{9,11},{10,... | collective-permute-start | bytes 393224 | tf_op jit(solution)/shard_map/ppermute | solution.py:292
  62.7 2.0 %collective-permute-start.18 = (bf16[128,512]{1,0:T(8,128)(2,1)S(1)}, bf16[128,512]{1,0:T(8,128)(2,1)S(1)}, u32[]{:S(2)}, u32[]{:S(2)}) collective-permute-start(bf16[128,512]{1,0:T(8,128)(2,1)S(1)} %shard_map.89.refs_1_), channel_id=1, source_target_pairs={{0,1},{1,0},{2,3},{3,2},{4,5},{5,4},{6,7},{7,6},{8,9},{9,8},{10,11... | collective-permute-start | bytes 393224 | tf_op jit(solution)/shard_map/ppermute | solution.py:292
  65.7 3.1 %collective-permute-done.16.refs_3_ = bf16[128,512]{1,0:T(8,128)(2,1)S(1)} collective-permute-done((bf16[128,512]{1,0:T(8,128)(2,1)S(1)}, bf16[128,512]{1,0:T(8,128)(2,1)S(1)}, u32[]{:S(2)}, u32[]{:S(2)}) %collective-permute-start.16) | collective-permute-done | bytes 131104 | tf_op jit(solution)/shard_map/ppermute | solution.py:292
  70.4 2.8 %collective-permute-done.18.refs_5_ = bf16[128,512]{1,0:T(8,128)(2,1)S(1)} collective-permute-done((bf16[128,512]{1,0:T(8,128)(2,1)S(1)}, bf16[128,512]{1,0:T(8,128)(2,1)S(1)}, u32[]{:S(2)}, u32[]{:S(2)}) %collective-permute-start.18) | collective-permute-done | bytes 131104 | tf_op jit(solution)/shard_map/ppermute | solution.py:292
  73.2 2.7 %collective-permute-done.21.refs_8_ = bf16[128,512]{1,0:T(8,128)(2,1)S(1)} collective-permute-done((bf16[128,512]{1,0:T(8,128)(2,1)S(1)}, bf16[128,512]{1,0:T(8,128)(2,1)S(1)}, u32[]{:S(2)}, u32[]{:S(2)}) %collective-permute-start.21) | collective-permute-done | bytes 131104 | tf_op jit(solution)/shard_map/ppermute | solution.py:292
  83.8 2.4 %collective-permute-done.24 = f32[64,512]{1,0:T(8,128)S(1)} collective-permute-done((f32[64,512]{1,0:T(8,128)S(1)}, f32[64,512]{1,0:T(8,128)S(1)}, u32[]{:S(2)}, u32[]{:S(2)}) %collective-permute-start.24) | collective-permute-done | bytes 131104 | tf_op jit(solution)/shard_map/ppermute | solution.py:295
  86.3 3.2 %collective-permute-done.26 = f32[64,512]{1,0:T(8,128)S(1)} collective-permute-done((f32[64,512]{1,0:T(8,128)S(1)}, f32[64,512]{1,0:T(8,128)S(1)}, u32[]{:S(2)}, u32[]{:S(2)}) %collective-permute-start.26) | collective-permute-done | bytes 131104 | tf_op jit(solution)/shard_map/ppermute | solution.py:295
  93.1 2.5 %collective-permute-done.30.refs_2_.refs_3_ = f32[64,512]{1,0:T(8,128)S(1)} collective-permute-done((f32[64,512]{1,0:T(8,128)S(1)}, f32[64,512]{1,0:T(8,128)S(1)}, u32[]{:S(2)}, u32[]{:S(2)}) %collective-permute-start.30) | collective-permute-done | bytes 131104 | tf_op jit(solution)/shard_map/ppermute | solution.py:295
  95.6 2.4 %collective-permute-done.32.refs_4_.refs_5_ = f32[64,512]{1,0:T(8,128)S(1)} collective-permute-done((f32[64,512]{1,0:T(8,128)S(1)}, f32[64,512]{1,0:T(8,128)S(1)}, u32[]{:S(2)}, u32[]{:S(2)}) %collective-permute-start.32) | collective-permute-done | bytes 131104 | tf_op jit(solution)/shard_map/ppermute | solution.py:295
  99.5 1.7 %shard_map.96 = (f32[2,64,512]{2,1,0:T(8,128)S(1)}, f32[2,64,512]{2,1,0:T(8,128)S(1)}) custom-call(s32[51]{0:T(128)S(1)} %concatenate.3.where, f32[256,512]{1,0:T(8,128)S(1)} %shard_map.95.refs_0_, f32[64,512]{1,0:T(8,128)S(1)} %add_add_fusion.refs_0_.refs_1_, f32[64,512]{1,0:T(8,128)S(1)} %collective-permute-done.29.refs_1_.refs_2_, ...), custom_call_target="tpu_custom_call" | custom-call | tf_op jit(solution)/shard_map/pallas_call | solution.py:263
  101.3 8.5 %collective-permute-done.45 = f32[2,64,512]{2,1,0:T(8,128)S(1)} collective-permute-done((f32[2,64,512]{2,1,0:T(8,128)S(1)}, f32[2,64,512]{2,1,0:T(8,128)S(1)}, u32[]{:S(2)}, u32[]{:S(2)}) %collective-permute-start.45) | collective-permute-done | bytes 262176 | tf_op jit(solution)/shard_map/ppermute | solution.py:292
  110.9 1.9 %shard_map.92 = f32[32,640]{1,0:T(8,128)S(1)} custom-call(s32[51]{0:T(128)S(1)} %concatenate.3.where, f32[64,512]{1,0:T(8,128)S(1)} %add_add_fusion.refs_0_.refs_1_, f32[64,512]{1,0:T(8,128)S(1)} %collective-permute-done.29.refs_1_.refs_2_, f32[64,512]{1,0:T(8,128)S(1)} %collective-permute-done.30.refs_2_.refs_3_, ...), custom_call_target="tpu_custom_call" | custom-call | tf_op jit(solution)/shard_map/pallas_call | solution.py:263
  114.3 9.9 %collective-permute-done.46 = f32[2,64,512]{2,1,0:T(8,128)S(1)} collective-permute-done((f32[2,64,512]{2,1,0:T(8,128)S(1)}, f32[2,64,512]{2,1,0:T(8,128)S(1)}, u32[]{:S(2)}, u32[]{:S(2)}) %collective-permute-start.46) | collective-permute-done | bytes 262176 | tf_op jit(solution)/shard_map/ppermute | solution.py:292
  124.3 2.2 %collective-permute-start.37 = (f32[32,640]{1,0:T(8,128)S(1)}, f32[32,640]{1,0:T(8,128)S(1)}, u32[]{:S(2)}, u32[]{:S(2)}) collective-permute-start(f32[32,640]{1,0:T(8,128)S(1)} %add.44), channel_id=1, source_target_pairs={{0,2},{1,3},{2,0},{3,1},{4,6},{5,7},{6,4},{7,5},{8,10},{9,11},{10,... | collective-permute-start | bytes 245768 | tf_op jit(solution)/shard_map/ppermute | solution.py:292
  126.5 5.5 %collective-permute-done.37 = f32[32,640]{1,0:T(8,128)S(1)} collective-permute-done((f32[32,640]{1,0:T(8,128)S(1)}, f32[32,640]{1,0:T(8,128)S(1)}, u32[]{:S(2)}, u32[]{:S(2)}) %collective-permute-start.37) | collective-permute-done | bytes 81952 | tf_op jit(solution)/shard_map/ppermute | solution.py:292
  132.6 1.7 %collective-permute-start.41 = (f32[32,640]{1,0:T(8,128)S(1)}, f32[32,640]{1,0:T(8,128)S(1)}, u32[]{:S(2)}, u32[]{:S(2)}) collective-permute-start(f32[32,640]{1,0:T(8,128)S(1)} %add.45.refs_0_), channel_id=1, source_target_pairs={{0,16},{4,20},{8,24},{12,28},{16,0},{20,4},{24,8},{28,12},{1,17},{... | collective-permute-start | bytes 245768 | tf_op jit(solution)/shard_map/ppermute | solution.py:295
  135.6 1.7 %collective-permute-done.39.refs_2_ = f32[32,640]{1,0:T(8,128)S(1)} collective-permute-done((f32[32,640]{1,0:T(8,128)S(1)}, f32[32,640]{1,0:T(8,128)S(1)}, u32[]{:S(2)}, u32[]{:S(2)}) %collective-permute-start.39) | collective-permute-done | bytes 81952 | tf_op jit(solution)/shard_map/ppermute | solution.py:295
  137.8 1.8 %collective-permute-done.43.refs_6_ = f32[32,640]{1,0:T(8,128)S(1)} collective-permute-done((f32[32,640]{1,0:T(8,128)S(1)}, f32[32,640]{1,0:T(8,128)S(1)}, u32[]{:S(2)}, u32[]{:S(2)}) %collective-permute-start.43) | collective-permute-done | bytes 81952 | tf_op jit(solution)/shard_map/ppermute | solution.py:295
  141.0 7.6 %shard_map.93.begun = f32[512,512]{1,0:T(8,128)S(1)} custom-call(s32[51]{0:T(128)S(1)} %concatenate.3.where, f32[32,640]{1,0:T(8,128)S(1)} %add.45.refs_0_, f32[32,640]{1,0:T(8,128)S(1)} %collective-permute-done.38.refs_1_, f32[32,640]{1,0:T(8,128)S(1)} %collective-permute-done.39.refs_2_, f32[32,640]{1,0:T(8,128)S(1)} %collective-permute-done.40.refs_3_, ...), custom_call_target="tpu_custom_call" | custom-call | tf_op jit(solution)/shard_map/pallas_call | solution.py:263
  148.6 8.5 %shard_map.94.refs_0_ = f32[512,512]{1,0:T(8,128)S(1)} custom-call(f32[512,512]{1,0:T(8,128)S(1)} %shard_map.93.begun), custom_call_target="tpu_custom_call" | custom-call | tf_op jit(solution)/shard_map/pallas_call | solution.py:263
  157.1 2.7 %shard_map.97 = (f32[64,512]{1,0:T(8,128)}, f32[256,512]{1,0:T(8,128)}) custom-call(s32[51]{0:T(128)S(1)} %concatenate.3.where, f32[512,512]{1,0:T(8,128)S(1)} %shard_map.94.refs_0_, f32[64,512]{1,0:T(8,128)S(1)} %add_add_fusion.refs_0_.refs_1_, f32[2,64,512]{2,1,0:T(8,128)S(1)} %add.47.refs_2_, f32[2,64,512]{2,1,0:T(8,128)S(1)} %collective-permute-done.47.refs_3_), custom_call_target="tpu_custom_call" | custom-call | tf_op jit(solution)/shard_map/pallas_call | solution.py:263
  (98 shorter events, 38.0 us)
Async XLA Ops:
  1.5 7.1 %collective-permute-start.3 = (bf16[64,512]{1,0:T(8,128)(2,1)S(1)}, bf16[64,512]{1,0:T(8,128)(2,1)S(1)}, u32[]{:S(2)}, u32[]{:S(2)}) collective-permute-start(bf16[64,512]{1,0:T(8,128)(2,1)S(1)} %constant_dynamic-slice_fusion), channel_id=1, source_target_pairs={{0,2},{1,3},{2,0},{3,1},{4,6},{5,7},{6,4},{7,5},{8,10},{9,11},{10,... | collective-permute-start | bytes 196616 | tf_op jit(solution)/shard_map/ppermute | solution.py:292
  7.1 6.1 %collective-permute-start.5 = (bf16[64,512]{1,0:T(8,128)(2,1)S(1)}, bf16[64,512]{1,0:T(8,128)(2,1)S(1)}, u32[]{:S(2)}, u32[]{:S(2)}) collective-permute-start(bf16[64,512]{1,0:T(8,128)(2,1)S(1)} %constant_dynamic-slice_fusion), channel_id=1, source_target_pairs={{0,3},{1,2},{2,1},{3,0},{4,7},{5,6},{6,5},{7,4},{8,11},{9,10},{10,... | collective-permute-start | bytes 196616 | tf_op jit(solution)/shard_map/ppermute | solution.py:292
  13.2 8.4 %collective-permute-start.9 = (bf16[3,64,512]{2,1,0:T(8,128)(2,1)S(1)}, bf16[3,64,512]{2,1,0:T(8,128)(2,1)S(1)}, u32[]{:S(2)}, u32[]{:S(2)}) collective-permute-start(bf16[3,64,512]{2,1,0:T(8,128)(2,1)S(1)} %pad_maximum_fusion.refs_0_), channel_id=1, source_target_pairs={{0,16},{4,20},{8,24},{12,28},{16,0},{20,4},{24,8},{28,12},{1,17},{... | collective-permute-start | bytes 589832 | tf_op jit(solution)/shard_map/ppermute | solution.py:295
  14.8 7.8 %collective-permute-start.11 = (bf16[3,64,512]{2,1,0:T(8,128)(2,1)S(1)}, bf16[3,64,512]{2,1,0:T(8,128)(2,1)S(1)}, u32[]{:S(2)}, u32[]{:S(2)}) collective-permute-start(bf16[3,64,512]{2,1,0:T(8,128)(2,1)S(1)} %pad_maximum_fusion.refs_0_), channel_id=1, source_target_pairs={{0,24},{4,28},{8,16},{12,20},{16,8},{20,12},{24,0},{28,4},{1,25},{... | collective-permute-start | bytes 589832 | tf_op jit(solution)/shard_map/ppermute | solution.py:295
  16.2 7.5 %collective-permute-start.7 = (bf16[3,64,512]{2,1,0:T(8,128)(2,1)S(1)}, bf16[3,64,512]{2,1,0:T(8,128)(2,1)S(1)}, u32[]{:S(2)}, u32[]{:S(2)}) collective-permute-start(bf16[3,64,512]{2,1,0:T(8,128)(2,1)S(1)} %pad_maximum_fusion.refs_0_), channel_id=1, source_target_pairs={{0,8},{4,12},{8,0},{12,4},{16,24},{20,28},{24,16},{28,20},{1,9},{5... | collective-permute-start | bytes 589832 | tf_op jit(solution)/shard_map/ppermute | solution.py:295
  16.8 20.2 %collective-permute-start.6 = (bf16[3,64,512]{2,1,0:T(8,128)(2,1)S(1)}, bf16[3,64,512]{2,1,0:T(8,128)(2,1)S(1)}, u32[]{:S(2)}, u32[]{:S(2)}) collective-permute-start(bf16[3,64,512]{2,1,0:T(8,128)(2,1)S(1)} %pad_maximum_fusion.refs_0_), channel_id=1, source_target_pairs={{0,4},{4,0},{8,12},{12,8},{16,20},{20,16},{24,28},{28,24},{1,5},{5... | collective-permute-start | bytes 589832 | tf_op jit(solution)/shard_map/ppermute | solution.py:295
  21.6 17.1 %collective-permute-start.10 = (bf16[3,64,512]{2,1,0:T(8,128)(2,1)S(1)}, bf16[3,64,512]{2,1,0:T(8,128)(2,1)S(1)}, u32[]{:S(2)}, u32[]{:S(2)}) collective-permute-start(bf16[3,64,512]{2,1,0:T(8,128)(2,1)S(1)} %collective-permute-done.9.refs_4_), channel_id=1, source_target_pairs={{0,4},{4,0},{8,12},{12,8},{16,20},{20,16},{24,28},{28,24},{1,5},{5... | collective-permute-start | bytes 589832 | tf_op jit(solution)/shard_map/ppermute | solution.py:295
  22.6 17.9 %collective-permute-start.12 = (bf16[3,64,512]{2,1,0:T(8,128)(2,1)S(1)}, bf16[3,64,512]{2,1,0:T(8,128)(2,1)S(1)}, u32[]{:S(2)}, u32[]{:S(2)}) collective-permute-start(bf16[3,64,512]{2,1,0:T(8,128)(2,1)S(1)} %collective-permute-done.11.refs_6_), channel_id=1, source_target_pairs={{0,4},{4,0},{8,12},{12,8},{16,20},{20,16},{24,28},{28,24},{1,5},{5... | collective-permute-start | bytes 589832 | tf_op jit(solution)/shard_map/ppermute | solution.py:295
  23.8 17.6 %collective-permute-start.8 = (bf16[3,64,512]{2,1,0:T(8,128)(2,1)S(1)}, bf16[3,64,512]{2,1,0:T(8,128)(2,1)S(1)}, u32[]{:S(2)}, u32[]{:S(2)}) collective-permute-start(bf16[3,64,512]{2,1,0:T(8,128)(2,1)S(1)} %collective-permute-done.7.refs_2_), channel_id=1, source_target_pairs={{0,4},{4,0},{8,12},{12,8},{16,20},{20,16},{24,28},{28,24},{1,5},{5... | collective-permute-start | bytes 589832 | tf_op jit(solution)/shard_map/ppermute | solution.py:295
  27.3 9.7 %collective-permute-start.13 = (bf16[128,512]{1,0:T(8,128)(2,1)S(1)}, bf16[128,512]{1,0:T(8,128)(2,1)S(1)}, u32[]{:S(2)}, u32[]{:S(2)}) collective-permute-start(bf16[128,512]{1,0:T(8,128)(2,1)S(1)} %get-tuple-element.25.refs_3_), channel_id=1, source_target_pairs={{0,2},{1,3},{2,0},{3,1},{4,6},{5,7},{6,4},{7,5},{8,10},{9,11},{10,... | collective-permute-start | bytes 393224 | tf_op jit(solution)/shard_map/ppermute | solution.py:292
  36.9 8.9 %collective-permute-start.14 = (bf16[128,512]{1,0:T(8,128)(2,1)S(1)}, bf16[128,512]{1,0:T(8,128)(2,1)S(1)}, u32[]{:S(2)}, u32[]{:S(2)}) collective-permute-start(bf16[128,512]{1,0:T(8,128)(2,1)S(1)} %get-tuple-element.27.refs_5_), channel_id=1, source_target_pairs={{0,1},{1,0},{2,3},{3,2},{4,5},{5,4},{6,7},{7,6},{8,9},{9,8},{10,11... | collective-permute-start | bytes 393224 | tf_op jit(solution)/shard_map/ppermute | solution.py:292
  36.9 8.9 %collective-permute-start.15 = (bf16[128,512]{1,0:T(8,128)(2,1)S(1)}, bf16[128,512]{1,0:T(8,128)(2,1)S(1)}, u32[]{:S(2)}, u32[]{:S(2)}) collective-permute-start(bf16[128,512]{1,0:T(8,128)(2,1)S(1)} %get-tuple-element.29.refs_7_), channel_id=1, source_target_pairs={{0,3},{1,2},{2,1},{3,0},{4,7},{5,6},{6,5},{7,4},{8,11},{9,10},{10,... | collective-permute-start | bytes 393224 | tf_op jit(solution)/shard_map/ppermute | solution.py:292
  38.7 19.8 %collective-permute-start = (bf16[128,512]{1,0:T(8,128)(2,1)S(1)}, bf16[128,512]{1,0:T(8,128)(2,1)S(1)}, u32[]{:S(2)}, u32[]{:S(2)}) collective-permute-start(bf16[128,512]{1,0:T(8,128)(2,1)S(1)} %get-tuple-element.24.refs_2_), channel_id=1, source_target_pairs={{0,2},{1,3},{2,0},{3,1},{4,6},{5,7},{6,4},{7,5},{8,10},{9,11},{10,... | collective-permute-start | bytes 393224 | tf_op jit(solution)/shard_map/ppermute | solution.py:292
  40.4 18.1 %collective-permute-start.1 = (bf16[128,512]{1,0:T(8,128)(2,1)S(1)}, bf16[128,512]{1,0:T(8,128)(2,1)S(1)}, u32[]{:S(2)}, u32[]{:S(2)}) collective-permute-start(bf16[128,512]{1,0:T(8,128)(2,1)S(1)} %get-tuple-element.26.refs_4_), channel_id=1, source_target_pairs={{0,1},{1,0},{2,3},{3,2},{4,5},{5,4},{6,7},{7,6},{8,9},{9,8},{10,11... | collective-permute-start | bytes 393224 | tf_op jit(solution)/shard_map/ppermute | solution.py:292
  41.4 17.2 %collective-permute-start.2 = (bf16[128,512]{1,0:T(8,128)(2,1)S(1)}, bf16[128,512]{1,0:T(8,128)(2,1)S(1)}, u32[]{:S(2)}, u32[]{:S(2)}) collective-permute-start(bf16[128,512]{1,0:T(8,128)(2,1)S(1)} %get-tuple-element.28.refs_6_), channel_id=1, source_target_pairs={{0,3},{1,2},{2,1},{3,0},{4,7},{5,6},{6,5},{7,4},{8,11},{9,10},{10,... | collective-permute-start | bytes 393224 | tf_op jit(solution)/shard_map/ppermute | solution.py:292
  46.3 19.4 %collective-permute-start.17 = (bf16[128,512]{1,0:T(8,128)(2,1)S(1)}, bf16[128,512]{1,0:T(8,128)(2,1)S(1)}, u32[]{:S(2)}, u32[]{:S(2)}) collective-permute-start(bf16[128,512]{1,0:T(8,128)(2,1)S(1)} %shard_map.90.refs_2_), channel_id=1, source_target_pairs={{0,2},{1,3},{2,0},{3,1},{4,6},{5,7},{6,4},{7,5},{8,10},{9,11},{10,... | collective-permute-start | bytes 393224 | tf_op jit(solution)/shard_map/ppermute | solution.py:292
  59.0 9.7 %collective-permute-start.16 = (bf16[128,512]{1,0:T(8,128)(2,1)S(1)}, bf16[128,512]{1,0:T(8,128)(2,1)S(1)}, u32[]{:S(2)}, u32[]{:S(2)}) collective-permute-start(bf16[128,512]{1,0:T(8,128)(2,1)S(1)} %shard_map.89.refs_1_), channel_id=1, source_target_pairs={{0,2},{1,3},{2,0},{3,1},{4,6},{5,7},{6,4},{7,5},{8,10},{9,11},{10,... | collective-permute-start | bytes 393224 | tf_op jit(solution)/shard_map/ppermute | solution.py:292
  62.7 7.7 %collective-permute-start.19 = (bf16[128,512]{1,0:T(8,128)(2,1)S(1)}, bf16[128,512]{1,0:T(8,128)(2,1)S(1)}, u32[]{:S(2)}, u32[]{:S(2)}) collective-permute-start(bf16[128,512]{1,0:T(8,128)(2,1)S(1)} %shard_map.90.refs_2_), channel_id=1, source_target_pairs={{0,1},{1,0},{2,3},{3,2},{4,5},{5,4},{6,7},{7,6},{8,9},{9,8},{10,11... | collective-permute-start | bytes 393224 | tf_op jit(solution)/shard_map/ppermute | solution.py:292
  62.7 10.5 %collective-permute-start.18 = (bf16[128,512]{1,0:T(8,128)(2,1)S(1)}, bf16[128,512]{1,0:T(8,128)(2,1)S(1)}, u32[]{:S(2)}, u32[]{:S(2)}) collective-permute-start(bf16[128,512]{1,0:T(8,128)(2,1)S(1)} %shard_map.89.refs_1_), channel_id=1, source_target_pairs={{0,1},{1,0},{2,3},{3,2},{4,5},{5,4},{6,7},{7,6},{8,9},{9,8},{10,11... | collective-permute-start | bytes 393224 | tf_op jit(solution)/shard_map/ppermute | solution.py:292
  65.7 10.2 %collective-permute-start.21 = (bf16[128,512]{1,0:T(8,128)(2,1)S(1)}, bf16[128,512]{1,0:T(8,128)(2,1)S(1)}, u32[]{:S(2)}, u32[]{:S(2)}) collective-permute-start(bf16[128,512]{1,0:T(8,128)(2,1)S(1)} %collective-permute-done.17.refs_4_), channel_id=1, source_target_pairs={{0,1},{1,0},{2,3},{3,2},{4,5},{5,4},{6,7},{7,6},{8,9},{9,8},{10,11... | collective-permute-start | bytes 393224 | tf_op jit(solution)/shard_map/ppermute | solution.py:292
  68.7 8.6 %collective-permute-start.20 = (bf16[128,512]{1,0:T(8,128)(2,1)S(1)}, bf16[128,512]{1,0:T(8,128)(2,1)S(1)}, u32[]{:S(2)}, u32[]{:S(2)}) collective-permute-start(bf16[128,512]{1,0:T(8,128)(2,1)S(1)} %collective-permute-done.16.refs_3_), channel_id=1, source_target_pairs={{0,1},{1,0},{2,3},{3,2},{4,5},{5,4},{6,7},{7,6},{8,9},{9,8},{10,11... | collective-permute-start | bytes 393224 | tf_op jit(solution)/shard_map/ppermute | solution.py:292
  80.1 6.2 %collective-permute-start.24 = (f32[64,512]{1,0:T(8,128)S(1)}, f32[64,512]{1,0:T(8,128)S(1)}, u32[]{:S(2)}, u32[]{:S(2)}) collective-permute-start(f32[64,512]{1,0:T(8,128)S(1)} %add.38), channel_id=1, source_target_pairs={{0,8},{4,12},{8,0},{12,4},{16,24},{20,28},{24,16},{28,20},{1,9},{5... | collective-permute-start | bytes 393224 | tf_op jit(solution)/shard_map/ppermute | solution.py:295
  81.3 8.1 %collective-permute-start.26 = (f32[64,512]{1,0:T(8,128)S(1)}, f32[64,512]{1,0:T(8,128)S(1)}, u32[]{:S(2)}, u32[]{:S(2)}) collective-permute-start(f32[64,512]{1,0:T(8,128)S(1)} %add.40), channel_id=1, source_target_pairs={{0,16},{4,20},{8,24},{12,28},{16,0},{20,4},{24,8},{28,12},{1,17},{... | collective-permute-start | bytes 393224 | tf_op jit(solution)/shard_map/ppermute | solution.py:295
  83.0 6.5 %collective-permute-start.28 = (f32[64,512]{1,0:T(8,128)S(1)}, f32[64,512]{1,0:T(8,128)S(1)}, u32[]{:S(2)}, u32[]{:S(2)}) collective-permute-start(f32[64,512]{1,0:T(8,128)S(1)} %add.42), channel_id=1, source_target_pairs={{0,24},{4,28},{8,16},{12,20},{16,8},{20,12},{24,0},{28,4},{1,25},{... | collective-permute-start | bytes 393224 | tf_op jit(solution)/shard_map/ppermute | solution.py:295
  90.8 7.2 %collective-permute-start.32 = (f32[64,512]{1,0:T(8,128)S(1)}, f32[64,512]{1,0:T(8,128)S(1)}, u32[]{:S(2)}, u32[]{:S(2)}) collective-permute-start(f32[64,512]{1,0:T(8,128)S(1)} %add_add_fusion.refs_0_.refs_1_), channel_id=1, source_target_pairs={{0,16},{4,20},{8,24},{12,28},{16,0},{20,4},{24,8},{28,12},{1,17},{... | collective-permute-start | bytes 393224 | tf_op jit(solution)/shard_map/ppermute | solution.py:295
  91.8 6.2 %collective-permute-start.34 = (f32[64,512]{1,0:T(8,128)S(1)}, f32[64,512]{1,0:T(8,128)S(1)}, u32[]{:S(2)}, u32[]{:S(2)}) collective-permute-start(f32[64,512]{1,0:T(8,128)S(1)} %add_add_fusion.refs_0_.refs_1_), channel_id=1, source_target_pairs={{0,24},{4,28},{8,16},{12,20},{16,8},{20,12},{24,0},{28,4},{1,25},{... | collective-permute-start | bytes 393224 | tf_op jit(solution)/shard_map/ppermute | solution.py:295
  93.1 6.3 %collective-permute-start.29 = (f32[64,512]{1,0:T(8,128)S(1)}, f32[64,512]{1,0:T(8,128)S(1)}, u32[]{:S(2)}, u32[]{:S(2)}) collective-permute-start(f32[64,512]{1,0:T(8,128)S(1)} %add_add_fusion.refs_0_.refs_1_), channel_id=1, source_target_pairs={{0,4},{4,0},{8,12},{12,8},{16,20},{20,16},{24,28},{28,24},{1,5},{5... | collective-permute-start | bytes 393224 | tf_op jit(solution)/shard_map/ppermute | solution.py:295
  101.2 8.6 %collective-permute-start.45 = (f32[2,64,512]{2,1,0:T(8,128)S(1)}, f32[2,64,512]{2,1,0:T(8,128)S(1)}, u32[]{:S(2)}, u32[]{:S(2)}) collective-permute-start(f32[2,64,512]{2,1,0:T(8,128)S(1)} %get-tuple-element.39), channel_id=1, source_target_pairs={{0,1},{1,0},{2,3},{3,2},{4,5},{5,4},{6,7},{7,6},{8,9},{9,8},{10,11... | collective-permute-start | bytes 786440 | tf_op jit(solution)/shard_map/ppermute | solution.py:292
  109.9 14.3 %collective-permute-start.46 = (f32[2,64,512]{2,1,0:T(8,128)S(1)}, f32[2,64,512]{2,1,0:T(8,128)S(1)}, u32[]{:S(2)}, u32[]{:S(2)}) collective-permute-start(f32[2,64,512]{2,1,0:T(8,128)S(1)} %rev.3), channel_id=1, source_target_pairs={{0,2},{1,3},{2,0},{3,1},{4,6},{5,7},{6,4},{7,5},{8,10},{9,11},{10,... | collective-permute-start | bytes 786440 | tf_op jit(solution)/shard_map/ppermute | solution.py:292
  112.7 11.5 %collective-permute-start.36 = (f32[32,640]{1,0:T(8,128)S(1)}, f32[32,640]{1,0:T(8,128)S(1)}, u32[]{:S(2)}, u32[]{:S(2)}) collective-permute-start(f32[32,640]{1,0:T(8,128)S(1)} %shard_map.92), channel_id=1, source_target_pairs={{0,1},{1,0},{2,3},{3,2},{4,5},{5,4},{6,7},{7,6},{8,9},{9,8},{10,11... | collective-permute-start | bytes 245768 | tf_op jit(solution)/shard_map/ppermute | solution.py:292
  124.2 32.9 %collective-permute-start.47 = (f32[2,64,512]{2,1,0:T(8,128)S(1)}, f32[2,64,512]{2,1,0:T(8,128)S(1)}, u32[]{:S(2)}, u32[]{:S(2)}) collective-permute-start(f32[2,64,512]{2,1,0:T(8,128)S(1)} %add.47.refs_2_), channel_id=1, source_target_pairs={{0,1},{1,0},{2,3},{3,2},{4,5},{5,4},{6,7},{7,6},{8,9},{9,8},{10,11... | collective-permute-start | bytes 786440 | tf_op jit(solution)/shard_map/ppermute | solution.py:292
  124.3 7.7 %collective-permute-start.37 = (f32[32,640]{1,0:T(8,128)S(1)}, f32[32,640]{1,0:T(8,128)S(1)}, u32[]{:S(2)}, u32[]{:S(2)}) collective-permute-start(f32[32,640]{1,0:T(8,128)S(1)} %add.44), channel_id=1, source_target_pairs={{0,2},{1,3},{2,0},{3,1},{4,6},{5,7},{6,4},{7,5},{8,10},{9,11},{10,... | collective-permute-start | bytes 245768 | tf_op jit(solution)/shard_map/ppermute | solution.py:292
  (20 other events, 108.6 us)

commit v3 on v2

--- a/solution.py
+++ b/solution.py
@@ -170,19 +170,23 @@
 
 def gram_kernel(where, places, *refs):
     pieces = refs[: len(places)]
-    gram, back, product = refs[len(places) :]
+    gram, back = refs[len(places) :]
     rows = pieces[0].shape[0]
     for i, piece in enumerate(pieces):
         back[i * rows : (i + 1) * rows, :] = piece[...]
     width = back.shape[1]
     band = gram.shape[0]
     bands = width // band
-    halves = []
+    tile_lanes = lax.broadcasted_iota(jnp.int32, (back.shape[0], TILE), 1)
+    sides = []
     for half, index in enumerate((where[1], bands - 1 - where[1])):
         start = index * band
         tile_at = pl.multiple_of(start // TILE * TILE, TILE)
-        product[half] = dot(back[:, pl.ds(tile_at, TILE)], back[...], ((0,), (0,)), precise)
-        halves.append(product[half, pl.ds(pl.multiple_of(start - tile_at, band), band), :])
+        shift = lax.rem(TILE + half * band - (start - tile_at), TILE)
+        sides.append(pltpu.roll(back[:, pl.ds(tile_at, TILE)], shift, 1))
+    left = jnp.where(tile_lanes < band, sides[0], sides[1])
+    product = dot(left, back[...], ((0,), (0,)), precise)
+    halves = [product[:band], product[band : 2 * band]]
     lead = where[1] * band // PANEL * PANEL
     turned = pltpu.roll(halves[1], lead, 1)
     lanes = lax.broadcasted_iota(jnp.int32, (band, width), 1)
@@ -366,7 +370,7 @@
     gram_rows = call(
         lambda where, *refs: gram_kernel(where, places, *refs),
         jax.ShapeDtypeStruct((band, width + TILE), f32),
-        [pltpu.VMEM((terms, width), f32), pltpu.VMEM((2, TILE, width), f32)],
+        [pltpu.VMEM((terms, width), f32)],
         [where],
         back_pieces,
     )

time: 160 us -> 160 us (level)
  no operation moved by 1% of the time
where the time goes in v3:
time: 160 us
  waiting for transfers between devices  80.7 us (50%)
  starting transfers between devices  47.6 us (30%)
  Pallas kernels  26.7 us (17%)
  local copies, waits for them, and re-layouts  2.94 us (2%)
    ppermute x20, waiting for transfers between devices, along(): return lax.ppermute(x, 'vocab', [(a, a ^ place) for a in range(n_vocab)])  57.8 us
    ppermute x20, starting transfers between devices, along(): return lax.ppermute(x, 'vocab', [(a, a ^ place) for a in range(n_vocab)])  31.3 us
    pallas_call x12, Pallas kernels, call(): pl.pallas_call(kernel, out_shape=outs, in_specs=[smem] * len(scalars) + [...  26.7 us
    ppermute x28, waiting for transfers between devices, across(): return lax.ppermute(x, 'doc', [(a, a ^ place) for a in range(n_doc)])  23 us
    ppermute x28, starting transfers between devices, across(): return lax.ppermute(x, 'doc', [(a, a ^ place) for a in range(n_doc)])  16.4 us
  transfers between devices with their start and end apart: 48, of which 28 were waited for; matrix products, arithmetic and copies ran while one was open for 1% of the time, Pallas kernels for 13%

profile of v3, /device:TPU:0, one launch (start us, length us, event | category | flops | bytes accessed | tf_op | source)
XLA Modules:
  0.0 159.8 jit_solution(16086220999118894176)
XLA Ops:
  1.5 4.1 %collective-permute-start.3 = (bf16[64,512]{1,0:T(8,128)(2,1)S(1)}, bf16[64,512]{1,0:T(8,128)(2,1)S(1)}, u32[]{:S(2)}, u32[]{:S(2)}) collective-permute-start(bf16[64,512]{1,0:T(8,128)(2,1)S(1)} %constant_dynamic-slice_fusion), channel_id=1, source_target_pairs={{0,2},{1,3},{2,0},{3,1},{4,6},{5,7},{6,4},{7,5},{8,10},{9,11},{10,... | collective-permute-start | bytes 196616 | tf_op jit(solution)/shard_map/ppermute | solution.py:296
  9.8 3.4 %collective-permute-done.5 = bf16[64,512]{1,0:T(8,128)(2,1)S(1)} collective-permute-done((bf16[64,512]{1,0:T(8,128)(2,1)S(1)}, bf16[64,512]{1,0:T(8,128)(2,1)S(1)}, u32[]{:S(2)}, u32[]{:S(2)}) %collective-permute-start.5) | collective-permute-done | bytes 65568 | tf_op jit(solution)/shard_map/ppermute | solution.py:296
  16.8 4.9 %collective-permute-done.9.refs_4_ = bf16[3,64,512]{2,1,0:T(8,128)(2,1)S(1)} collective-permute-done((bf16[3,64,512]{2,1,0:T(8,128)(2,1)S(1)}, bf16[3,64,512]{2,1,0:T(8,128)(2,1)S(1)}, u32[]{:S(2)}, u32[]{:S(2)}) %collective-permute-start.9) | collective-permute-done | bytes 196640 | tf_op jit(solution)/shard_map/ppermute | solution.py:299
  27.3 2.6 %collective-permute-start.13 = (bf16[128,512]{1,0:T(8,128)(2,1)S(1)}, bf16[128,512]{1,0:T(8,128)(2,1)S(1)}, u32[]{:S(2)}, u32[]{:S(2)}) collective-permute-start(bf16[128,512]{1,0:T(8,128)(2,1)S(1)} %get-tuple-element.25.refs_3_), channel_id=1, source_target_pairs={{0,2},{1,3},{2,0},{3,1},{4,6},{5,7},{6,4},{7,5},{8,10},{9,11},{10,... | collective-permute-start | bytes 393224 | tf_op jit(solution)/shard_map/ppermute | solution.py:296
  29.9 7.0 %collective-permute-done.13.refs_1_ = bf16[128,512]{1,0:T(8,128)(2,1)S(1)} collective-permute-done((bf16[128,512]{1,0:T(8,128)(2,1)S(1)}, bf16[128,512]{1,0:T(8,128)(2,1)S(1)}, u32[]{:S(2)}, u32[]{:S(2)}) %collective-permute-start.13) | collective-permute-done | bytes 131104 | tf_op jit(solution)/shard_map/ppermute | solution.py:296
  36.9 1.8 %collective-permute-start.15 = (bf16[128,512]{1,0:T(8,128)(2,1)S(1)}, bf16[128,512]{1,0:T(8,128)(2,1)S(1)}, u32[]{:S(2)}, u32[]{:S(2)}) collective-permute-start(bf16[128,512]{1,0:T(8,128)(2,1)S(1)} %get-tuple-element.29.refs_7_), channel_id=1, source_target_pairs={{0,3},{1,2},{2,1},{3,0},{4,7},{5,6},{6,5},{7,4},{8,11},{9,10},{10,... | collective-permute-start | bytes 393224 | tf_op jit(solution)/shard_map/ppermute | solution.py:296
  38.7 1.7 %collective-permute-start = (bf16[128,512]{1,0:T(8,128)(2,1)S(1)}, bf16[128,512]{1,0:T(8,128)(2,1)S(1)}, u32[]{:S(2)}, u32[]{:S(2)}) collective-permute-start(bf16[128,512]{1,0:T(8,128)(2,1)S(1)} %get-tuple-element.24.refs_2_), channel_id=1, source_target_pairs={{0,2},{1,3},{2,0},{3,1},{4,6},{5,7},{6,4},{7,5},{8,10},{9,11},{10,... | collective-permute-start | bytes 393224 | tf_op jit(solution)/shard_map/ppermute | solution.py:296
  41.4 1.8 %collective-permute-start.2 = (bf16[128,512]{1,0:T(8,128)(2,1)S(1)}, bf16[128,512]{1,0:T(8,128)(2,1)S(1)}, u32[]{:S(2)}, u32[]{:S(2)}) collective-permute-start(bf16[128,512]{1,0:T(8,128)(2,1)S(1)} %get-tuple-element.28.refs_6_), channel_id=1, source_target_pairs={{0,3},{1,2},{2,1},{3,0},{4,7},{5,6},{6,5},{7,4},{8,11},{9,10},{10,... | collective-permute-start | bytes 393224 | tf_op jit(solution)/shard_map/ppermute | solution.py:296
  43.8 2.0 %collective-permute-done.14.refs_2_ = bf16[128,512]{1,0:T(8,128)(2,1)S(1)} collective-permute-done((bf16[128,512]{1,0:T(8,128)(2,1)S(1)}, bf16[128,512]{1,0:T(8,128)(2,1)S(1)}, u32[]{:S(2)}, u32[]{:S(2)}) %collective-permute-start.14) | collective-permute-done | bytes 131104 | tf_op jit(solution)/shard_map/ppermute | solution.py:296
  46.3 5.2 %collective-permute-start.17 = (bf16[128,512]{1,0:T(8,128)(2,1)S(1)}, bf16[128,512]{1,0:T(8,128)(2,1)S(1)}, u32[]{:S(2)}, u32[]{:S(2)}) collective-permute-start(bf16[128,512]{1,0:T(8,128)(2,1)S(1)} %shard_map.90.refs_2_), channel_id=1, source_target_pairs={{0,2},{1,3},{2,0},{3,1},{4,6},{5,7},{6,4},{7,5},{8,10},{9,11},{10,... | collective-permute-start | bytes 393224 | tf_op jit(solution)/shard_map/ppermute | solution.py:296
  51.5 7.0 %collective-permute-done.refs_1_ = bf16[128,512]{1,0:T(8,128)(2,1)S(1)} collective-permute-done((bf16[128,512]{1,0:T(8,128)(2,1)S(1)}, bf16[128,512]{1,0:T(8,128)(2,1)S(1)}, u32[]{:S(2)}, u32[]{:S(2)}) %collective-permute-start) | collective-permute-done | bytes 131104 | tf_op jit(solution)/shard_map/ppermute | solution.py:296
  59.0 3.7 %collective-permute-start.16 = (bf16[128,512]{1,0:T(8,128)(2,1)S(1)}, bf16[128,512]{1,0:T(8,128)(2,1)S(1)}, u32[]{:S(2)}, u32[]{:S(2)}) collective-permute-start(bf16[128,512]{1,0:T(8,128)(2,1)S(1)} %shard_map.89.refs_1_), channel_id=1, source_target_pairs={{0,2},{1,3},{2,0},{3,1},{4,6},{5,7},{6,4},{7,5},{8,10},{9,11},{10,... | collective-permute-start | bytes 393224 | tf_op jit(solution)/shard_map/ppermute | solution.py:296
  62.7 2.0 %collective-permute-start.18 = (bf16[128,512]{1,0:T(8,128)(2,1)S(1)}, bf16[128,512]{1,0:T(8,128)(2,1)S(1)}, u32[]{:S(2)}, u32[]{:S(2)}) collective-permute-start(bf16[128,512]{1,0:T(8,128)(2,1)S(1)} %shard_map.89.refs_1_), channel_id=1, source_target_pairs={{0,1},{1,0},{2,3},{3,2},{4,5},{5,4},{6,7},{7,6},{8,9},{9,8},{10,11... | collective-permute-start | bytes 393224 | tf_op jit(solution)/shard_map/ppermute | solution.py:296
  65.7 3.1 %collective-permute-done.16.refs_3_ = bf16[128,512]{1,0:T(8,128)(2,1)S(1)} collective-permute-done((bf16[128,512]{1,0:T(8,128)(2,1)S(1)}, bf16[128,512]{1,0:T(8,128)(2,1)S(1)}, u32[]{:S(2)}, u32[]{:S(2)}) %collective-permute-start.16) | collective-permute-done | bytes 131104 | tf_op jit(solution)/shard_map/ppermute | solution.py:296
  70.4 2.8 %collective-permute-done.18.refs_5_ = bf16[128,512]{1,0:T(8,128)(2,1)S(1)} collective-permute-done((bf16[128,512]{1,0:T(8,128)(2,1)S(1)}, bf16[128,512]{1,0:T(8,128)(2,1)S(1)}, u32[]{:S(2)}, u32[]{:S(2)}) %collective-permute-start.18) | collective-permute-done | bytes 131104 | tf_op jit(solution)/shard_map/ppermute | solution.py:296
  73.2 2.7 %collective-permute-done.21.refs_8_ = bf16[128,512]{1,0:T(8,128)(2,1)S(1)} collective-permute-done((bf16[128,512]{1,0:T(8,128)(2,1)S(1)}, bf16[128,512]{1,0:T(8,128)(2,1)S(1)}, u32[]{:S(2)}, u32[]{:S(2)}) %collective-permute-start.21) | collective-permute-done | bytes 131104 | tf_op jit(solution)/shard_map/ppermute | solution.py:296
  81.3 1.6 %collective-permute-start.26 = (f32[64,512]{1,0:T(8,128)S(1)}, f32[64,512]{1,0:T(8,128)S(1)}, u32[]{:S(2)}, u32[]{:S(2)}) collective-permute-start(f32[64,512]{1,0:T(8,128)S(1)} %add.40), channel_id=1, source_target_pairs={{0,16},{4,20},{8,24},{12,28},{16,0},{20,4},{24,8},{28,12},{1,17},{... | collective-permute-start | bytes 393224 | tf_op jit(solution)/shard_map/ppermute | solution.py:299
  83.8 2.4 %collective-permute-done.24 = f32[64,512]{1,0:T(8,128)S(1)} collective-permute-done((f32[64,512]{1,0:T(8,128)S(1)}, f32[64,512]{1,0:T(8,128)S(1)}, u32[]{:S(2)}, u32[]{:S(2)}) %collective-permute-start.24) | collective-permute-done | bytes 131104 | tf_op jit(solution)/shard_map/ppermute | solution.py:299
  86.3 3.2 %collective-permute-done.26 = f32[64,512]{1,0:T(8,128)S(1)} collective-permute-done((f32[64,512]{1,0:T(8,128)S(1)}, f32[64,512]{1,0:T(8,128)S(1)}, u32[]{:S(2)}, u32[]{:S(2)}) %collective-permute-start.26) | collective-permute-done | bytes 131104 | tf_op jit(solution)/shard_map/ppermute | solution.py:299
  93.1 2.5 %collective-permute-done.30.refs_2_.refs_3_ = f32[64,512]{1,0:T(8,128)S(1)} collective-permute-done((f32[64,512]{1,0:T(8,128)S(1)}, f32[64,512]{1,0:T(8,128)S(1)}, u32[]{:S(2)}, u32[]{:S(2)}) %collective-permute-start.30) | collective-permute-done | bytes 131104 | tf_op jit(solution)/shard_map/ppermute | solution.py:299
  95.6 2.4 %collective-permute-done.32.refs_4_.refs_5_ = f32[64,512]{1,0:T(8,128)S(1)} collective-permute-done((f32[64,512]{1,0:T(8,128)S(1)}, f32[64,512]{1,0:T(8,128)S(1)}, u32[]{:S(2)}, u32[]{:S(2)}) %collective-permute-start.32) | collective-permute-done | bytes 131104 | tf_op jit(solution)/shard_map/ppermute | solution.py:299
  99.5 1.7 %shard_map.96 = (f32[2,64,512]{2,1,0:T(8,128)S(1)}, f32[2,64,512]{2,1,0:T(8,128)S(1)}) custom-call(s32[51]{0:T(128)S(1)} %concatenate.3.where, f32[256,512]{1,0:T(8,128)S(1)} %shard_map.95.refs_0_, f32[64,512]{1,0:T(8,128)S(1)} %add_add_fusion.refs_0_.refs_1_, f32[64,512]{1,0:T(8,128)S(1)} %collective-permute-done.29.refs_1_.refs_2_, ...), custom_call_target="tpu_custom_call" | custom-call | tf_op jit(solution)/shard_map/pallas_call | solution.py:267
  101.3 8.5 %collective-permute-done.45 = f32[2,64,512]{2,1,0:T(8,128)S(1)} collective-permute-done((f32[2,64,512]{2,1,0:T(8,128)S(1)}, f32[2,64,512]{2,1,0:T(8,128)S(1)}, u32[]{:S(2)}, u32[]{:S(2)}) %collective-permute-start.45) | collective-permute-done | bytes 262176 | tf_op jit(solution)/shard_map/ppermute | solution.py:296
  113.8 10.3 %collective-permute-done.46 = f32[2,64,512]{2,1,0:T(8,128)S(1)} collective-permute-done((f32[2,64,512]{2,1,0:T(8,128)S(1)}, f32[2,64,512]{2,1,0:T(8,128)S(1)}, u32[]{:S(2)}, u32[]{:S(2)}) %collective-permute-start.46) | collective-permute-done | bytes 262176 | tf_op jit(solution)/shard_map/ppermute | solution.py:296
  124.3 2.2 %collective-permute-start.37 = (f32[32,640]{1,0:T(8,128)S(1)}, f32[32,640]{1,0:T(8,128)S(1)}, u32[]{:S(2)}, u32[]{:S(2)}) collective-permute-start(f32[32,640]{1,0:T(8,128)S(1)} %add.44), channel_id=1, source_target_pairs={{0,2},{1,3},{2,0},{3,1},{4,6},{5,7},{6,4},{7,5},{8,10},{9,11},{10,... | collective-permute-start | bytes 245768 | tf_op jit(solution)/shard_map/ppermute | solution.py:296
  126.5 5.5 %collective-permute-done.37 = f32[32,640]{1,0:T(8,128)S(1)} collective-permute-done((f32[32,640]{1,0:T(8,128)S(1)}, f32[32,640]{1,0:T(8,128)S(1)}, u32[]{:S(2)}, u32[]{:S(2)}) %collective-permute-start.37) | collective-permute-done | bytes 81952 | tf_op jit(solution)/shard_map/ppermute | solution.py:296
  132.6 1.7 %collective-permute-start.41 = (f32[32,640]{1,0:T(8,128)S(1)}, f32[32,640]{1,0:T(8,128)S(1)}, u32[]{:S(2)}, u32[]{:S(2)}) collective-permute-start(f32[32,640]{1,0:T(8,128)S(1)} %add.45.refs_0_), channel_id=1, source_target_pairs={{0,16},{4,20},{8,24},{12,28},{16,0},{20,4},{24,8},{28,12},{1,17},{... | collective-permute-start | bytes 245768 | tf_op jit(solution)/shard_map/ppermute | solution.py:299
  135.6 1.7 %collective-permute-done.39.refs_2_ = f32[32,640]{1,0:T(8,128)S(1)} collective-permute-done((f32[32,640]{1,0:T(8,128)S(1)}, f32[32,640]{1,0:T(8,128)S(1)}, u32[]{:S(2)}, u32[]{:S(2)}) %collective-permute-start.39) | collective-permute-done | bytes 81952 | tf_op jit(solution)/shard_map/ppermute | solution.py:299
  137.8 1.8 %collective-permute-done.43.refs_6_ = f32[32,640]{1,0:T(8,128)S(1)} collective-permute-done((f32[32,640]{1,0:T(8,128)S(1)}, f32[32,640]{1,0:T(8,128)S(1)}, u32[]{:S(2)}, u32[]{:S(2)}) %collective-permute-start.43) | collective-permute-done | bytes 81952 | tf_op jit(solution)/shard_map/ppermute | solution.py:299
  141.0 7.6 %shard_map.93.begun = f32[512,512]{1,0:T(8,128)S(1)} custom-call(s32[51]{0:T(128)S(1)} %concatenate.3.where, f32[32,640]{1,0:T(8,128)S(1)} %add.45.refs_0_, f32[32,640]{1,0:T(8,128)S(1)} %collective-permute-done.38.refs_1_, f32[32,640]{1,0:T(8,128)S(1)} %collective-permute-done.39.refs_2_, f32[32,640]{1,0:T(8,128)S(1)} %collective-permute-done.40.refs_3_, ...), custom_call_target="tpu_custom_call" | custom-call | tf_op jit(solution)/shard_map/pallas_call | solution.py:267
  148.6 8.5 %shard_map.94.refs_0_ = f32[512,512]{1,0:T(8,128)S(1)} custom-call(f32[512,512]{1,0:T(8,128)S(1)} %shard_map.93.begun), custom_call_target="tpu_custom_call" | custom-call | tf_op jit(solution)/shard_map/pallas_call | solution.py:267
  157.1 2.7 %shard_map.97 = (f32[64,512]{1,0:T(8,128)}, f32[256,512]{1,0:T(8,128)}) custom-call(s32[51]{0:T(128)S(1)} %concatenate.3.where, f32[512,512]{1,0:T(8,128)S(1)} %shard_map.94.refs_0_, f32[64,512]{1,0:T(8,128)S(1)} %add_add_fusion.refs_0_.refs_1_, f32[2,64,512]{2,1,0:T(8,128)S(1)} %add.47.refs_2_, f32[2,64,512]{2,1,0:T(8,128)S(1)} %collective-permute-done.47.refs_3_), custom_call_target="tpu_custom_call" | custom-call | tf_op jit(solution)/shard_map/pallas_call | solution.py:267
  (98 shorter events, 37.8 us)
Async XLA Ops:
  1.5 7.1 %collective-permute-start.3 = (bf16[64,512]{1,0:T(8,128)(2,1)S(1)}, bf16[64,512]{1,0:T(8,128)(2,1)S(1)}, u32[]{:S(2)}, u32[]{:S(2)}) collective-permute-start(bf16[64,512]{1,0:T(8,128)(2,1)S(1)} %constant_dynamic-slice_fusion), channel_id=1, source_target_pairs={{0,2},{1,3},{2,0},{3,1},{4,6},{5,7},{6,4},{7,5},{8,10},{9,11},{10,... | collective-permute-start | bytes 196616 | tf_op jit(solution)/shard_map/ppermute | solution.py:296
  7.1 6.1 %collective-permute-start.5 = (bf16[64,512]{1,0:T(8,128)(2,1)S(1)}, bf16[64,512]{1,0:T(8,128)(2,1)S(1)}, u32[]{:S(2)}, u32[]{:S(2)}) collective-permute-start(bf16[64,512]{1,0:T(8,128)(2,1)S(1)} %constant_dynamic-slice_fusion), channel_id=1, source_target_pairs={{0,3},{1,2},{2,1},{3,0},{4,7},{5,6},{6,5},{7,4},{8,11},{9,10},{10,... | collective-permute-start | bytes 196616 | tf_op jit(solution)/shard_map/ppermute | solution.py:296
  13.2 8.4 %collective-permute-start.9 = (bf16[3,64,512]{2,1,0:T(8,128)(2,1)S(1)}, bf16[3,64,512]{2,1,0:T(8,128)(2,1)S(1)}, u32[]{:S(2)}, u32[]{:S(2)}) collective-permute-start(bf16[3,64,512]{2,1,0:T(8,128)(2,1)S(1)} %pad_maximum_fusion.refs_0_), channel_id=1, source_target_pairs={{0,16},{4,20},{8,24},{12,28},{16,0},{20,4},{24,8},{28,12},{1,17},{... | collective-permute-start | bytes 589832 | tf_op jit(solution)/shard_map/ppermute | solution.py:299
  14.8 7.8 %collective-permute-start.11 = (bf16[3,64,512]{2,1,0:T(8,128)(2,1)S(1)}, bf16[3,64,512]{2,1,0:T(8,128)(2,1)S(1)}, u32[]{:S(2)}, u32[]{:S(2)}) collective-permute-start(bf16[3,64,512]{2,1,0:T(8,128)(2,1)S(1)} %pad_maximum_fusion.refs_0_), channel_id=1, source_target_pairs={{0,24},{4,28},{8,16},{12,20},{16,8},{20,12},{24,0},{28,4},{1,25},{... | collective-permute-start | bytes 589832 | tf_op jit(solution)/shard_map/ppermute | solution.py:299
  16.2 7.5 %collective-permute-start.7 = (bf16[3,64,512]{2,1,0:T(8,128)(2,1)S(1)}, bf16[3,64,512]{2,1,0:T(8,128)(2,1)S(1)}, u32[]{:S(2)}, u32[]{:S(2)}) collective-permute-start(bf16[3,64,512]{2,1,0:T(8,128)(2,1)S(1)} %pad_maximum_fusion.refs_0_), channel_id=1, source_target_pairs={{0,8},{4,12},{8,0},{12,4},{16,24},{20,28},{24,16},{28,20},{1,9},{5... | collective-permute-start | bytes 589832 | tf_op jit(solution)/shard_map/ppermute | solution.py:299
  16.8 20.2 %collective-permute-start.6 = (bf16[3,64,512]{2,1,0:T(8,128)(2,1)S(1)}, bf16[3,64,512]{2,1,0:T(8,128)(2,1)S(1)}, u32[]{:S(2)}, u32[]{:S(2)}) collective-permute-start(bf16[3,64,512]{2,1,0:T(8,128)(2,1)S(1)} %pad_maximum_fusion.refs_0_), channel_id=1, source_target_pairs={{0,4},{4,0},{8,12},{12,8},{16,20},{20,16},{24,28},{28,24},{1,5},{5... | collective-permute-start | bytes 589832 | tf_op jit(solution)/shard_map/ppermute | solution.py:299
  21.6 17.1 %collective-permute-start.10 = (bf16[3,64,512]{2,1,0:T(8,128)(2,1)S(1)}, bf16[3,64,512]{2,1,0:T(8,128)(2,1)S(1)}, u32[]{:S(2)}, u32[]{:S(2)}) collective-permute-start(bf16[3,64,512]{2,1,0:T(8,128)(2,1)S(1)} %collective-permute-done.9.refs_4_), channel_id=1, source_target_pairs={{0,4},{4,0},{8,12},{12,8},{16,20},{20,16},{24,28},{28,24},{1,5},{5... | collective-permute-start | bytes 589832 | tf_op jit(solution)/shard_map/ppermute | solution.py:299
  22.6 17.9 %collective-permute-start.12 = (bf16[3,64,512]{2,1,0:T(8,128)(2,1)S(1)}, bf16[3,64,512]{2,1,0:T(8,128)(2,1)S(1)}, u32[]{:S(2)}, u32[]{:S(2)}) collective-permute-start(bf16[3,64,512]{2,1,0:T(8,128)(2,1)S(1)} %collective-permute-done.11.refs_6_), channel_id=1, source_target_pairs={{0,4},{4,0},{8,12},{12,8},{16,20},{20,16},{24,28},{28,24},{1,5},{5... | collective-permute-start | bytes 589832 | tf_op jit(solution)/shard_map/ppermute | solution.py:299
  23.8 17.6 %collective-permute-start.8 = (bf16[3,64,512]{2,1,0:T(8,128)(2,1)S(1)}, bf16[3,64,512]{2,1,0:T(8,128)(2,1)S(1)}, u32[]{:S(2)}, u32[]{:S(2)}) collective-permute-start(bf16[3,64,512]{2,1,0:T(8,128)(2,1)S(1)} %collective-permute-done.7.refs_2_), channel_id=1, source_target_pairs={{0,4},{4,0},{8,12},{12,8},{16,20},{20,16},{24,28},{28,24},{1,5},{5... | collective-permute-start | bytes 589832 | tf_op jit(solution)/shard_map/ppermute | solution.py:299
  27.3 9.7 %collective-permute-start.13 = (bf16[128,512]{1,0:T(8,128)(2,1)S(1)}, bf16[128,512]{1,0:T(8,128)(2,1)S(1)}, u32[]{:S(2)}, u32[]{:S(2)}) collective-permute-start(bf16[128,512]{1,0:T(8,128)(2,1)S(1)} %get-tuple-element.25.refs_3_), channel_id=1, source_target_pairs={{0,2},{1,3},{2,0},{3,1},{4,6},{5,7},{6,4},{7,5},{8,10},{9,11},{10,... | collective-permute-start | bytes 393224 | tf_op jit(solution)/shard_map/ppermute | solution.py:296
  36.9 8.9 %collective-permute-start.14 = (bf16[128,512]{1,0:T(8,128)(2,1)S(1)}, bf16[128,512]{1,0:T(8,128)(2,1)S(1)}, u32[]{:S(2)}, u32[]{:S(2)}) collective-permute-start(bf16[128,512]{1,0:T(8,128)(2,1)S(1)} %get-tuple-element.27.refs_5_), channel_id=1, source_target_pairs={{0,1},{1,0},{2,3},{3,2},{4,5},{5,4},{6,7},{7,6},{8,9},{9,8},{10,11... | collective-permute-start | bytes 393224 | tf_op jit(solution)/shard_map/ppermute | solution.py:296
  36.9 8.9 %collective-permute-start.15 = (bf16[128,512]{1,0:T(8,128)(2,1)S(1)}, bf16[128,512]{1,0:T(8,128)(2,1)S(1)}, u32[]{:S(2)}, u32[]{:S(2)}) collective-permute-start(bf16[128,512]{1,0:T(8,128)(2,1)S(1)} %get-tuple-element.29.refs_7_), channel_id=1, source_target_pairs={{0,3},{1,2},{2,1},{3,0},{4,7},{5,6},{6,5},{7,4},{8,11},{9,10},{10,... | collective-permute-start | bytes 393224 | tf_op jit(solution)/shard_map/ppermute | solution.py:296
  38.7 19.8 %collective-permute-start = (bf16[128,512]{1,0:T(8,128)(2,1)S(1)}, bf16[128,512]{1,0:T(8,128)(2,1)S(1)}, u32[]{:S(2)}, u32[]{:S(2)}) collective-permute-start(bf16[128,512]{1,0:T(8,128)(2,1)S(1)} %get-tuple-element.24.refs_2_), channel_id=1, source_target_pairs={{0,2},{1,3},{2,0},{3,1},{4,6},{5,7},{6,4},{7,5},{8,10},{9,11},{10,... | collective-permute-start | bytes 393224 | tf_op jit(solution)/shard_map/ppermute | solution.py:296
  40.4 18.1 %collective-permute-start.1 = (bf16[128,512]{1,0:T(8,128)(2,1)S(1)}, bf16[128,512]{1,0:T(8,128)(2,1)S(1)}, u32[]{:S(2)}, u32[]{:S(2)}) collective-permute-start(bf16[128,512]{1,0:T(8,128)(2,1)S(1)} %get-tuple-element.26.refs_4_), channel_id=1, source_target_pairs={{0,1},{1,0},{2,3},{3,2},{4,5},{5,4},{6,7},{7,6},{8,9},{9,8},{10,11... | collective-permute-start | bytes 393224 | tf_op jit(solution)/shard_map/ppermute | solution.py:296
  41.4 17.2 %collective-permute-start.2 = (bf16[128,512]{1,0:T(8,128)(2,1)S(1)}, bf16[128,512]{1,0:T(8,128)(2,1)S(1)}, u32[]{:S(2)}, u32[]{:S(2)}) collective-permute-start(bf16[128,512]{1,0:T(8,128)(2,1)S(1)} %get-tuple-element.28.refs_6_), channel_id=1, source_target_pairs={{0,3},{1,2},{2,1},{3,0},{4,7},{5,6},{6,5},{7,4},{8,11},{9,10},{10,... | collective-permute-start | bytes 393224 | tf_op jit(solution)/shard_map/ppermute | solution.py:296
  46.3 19.4 %collective-permute-start.17 = (bf16[128,512]{1,0:T(8,128)(2,1)S(1)}, bf16[128,512]{1,0:T(8,128)(2,1)S(1)}, u32[]{:S(2)}, u32[]{:S(2)}) collective-permute-start(bf16[128,512]{1,0:T(8,128)(2,1)S(1)} %shard_map.90.refs_2_), channel_id=1, source_target_pairs={{0,2},{1,3},{2,0},{3,1},{4,6},{5,7},{6,4},{7,5},{8,10},{9,11},{10,... | collective-permute-start | bytes 393224 | tf_op jit(solution)/shard_map/ppermute | solution.py:296
  59.0 9.7 %collective-permute-start.16 = (bf16[128,512]{1,0:T(8,128)(2,1)S(1)}, bf16[128,512]{1,0:T(8,128)(2,1)S(1)}, u32[]{:S(2)}, u32[]{:S(2)}) collective-permute-start(bf16[128,512]{1,0:T(8,128)(2,1)S(1)} %shard_map.89.refs_1_), channel_id=1, source_target_pairs={{0,2},{1,3},{2,0},{3,1},{4,6},{5,7},{6,4},{7,5},{8,10},{9,11},{10,... | collective-permute-start | bytes 393224 | tf_op jit(solution)/shard_map/ppermute | solution.py:296
  62.7 7.7 %collective-permute-start.19 = (bf16[128,512]{1,0:T(8,128)(2,1)S(1)}, bf16[128,512]{1,0:T(8,128)(2,1)S(1)}, u32[]{:S(2)}, u32[]{:S(2)}) collective-permute-start(bf16[128,512]{1,0:T(8,128)(2,1)S(1)} %shard_map.90.refs_2_), channel_id=1, source_target_pairs={{0,1},{1,0},{2,3},{3,2},{4,5},{5,4},{6,7},{7,6},{8,9},{9,8},{10,11... | collective-permute-start | bytes 393224 | tf_op jit(solution)/shard_map/ppermute | solution.py:296
  62.7 10.5 %collective-permute-start.18 = (bf16[128,512]{1,0:T(8,128)(2,1)S(1)}, bf16[128,512]{1,0:T(8,128)(2,1)S(1)}, u32[]{:S(2)}, u32[]{:S(2)}) collective-permute-start(bf16[128,512]{1,0:T(8,128)(2,1)S(1)} %shard_map.89.refs_1_), channel_id=1, source_target_pairs={{0,1},{1,0},{2,3},{3,2},{4,5},{5,4},{6,7},{7,6},{8,9},{9,8},{10,11... | collective-permute-start | bytes 393224 | tf_op jit(solution)/shard_map/ppermute | solution.py:296
  65.7 10.2 %collective-permute-start.21 = (bf16[128,512]{1,0:T(8,128)(2,1)S(1)}, bf16[128,512]{1,0:T(8,128)(2,1)S(1)}, u32[]{:S(2)}, u32[]{:S(2)}) collective-permute-start(bf16[128,512]{1,0:T(8,128)(2,1)S(1)} %collective-permute-done.17.refs_4_), channel_id=1, source_target_pairs={{0,1},{1,0},{2,3},{3,2},{4,5},{5,4},{6,7},{7,6},{8,9},{9,8},{10,11... | collective-permute-start | bytes 393224 | tf_op jit(solution)/shard_map/ppermute | solution.py:296
  68.7 8.6 %collective-permute-start.20 = (bf16[128,512]{1,0:T(8,128)(2,1)S(1)}, bf16[128,512]{1,0:T(8,128)(2,1)S(1)}, u32[]{:S(2)}, u32[]{:S(2)}) collective-permute-start(bf16[128,512]{1,0:T(8,128)(2,1)S(1)} %collective-permute-done.16.refs_3_), channel_id=1, source_target_pairs={{0,1},{1,0},{2,3},{3,2},{4,5},{5,4},{6,7},{7,6},{8,9},{9,8},{10,11... | collective-permute-start | bytes 393224 | tf_op jit(solution)/shard_map/ppermute | solution.py:296
  80.1 6.2 %collective-permute-start.24 = (f32[64,512]{1,0:T(8,128)S(1)}, f32[64,512]{1,0:T(8,128)S(1)}, u32[]{:S(2)}, u32[]{:S(2)}) collective-permute-start(f32[64,512]{1,0:T(8,128)S(1)} %add.38), channel_id=1, source_target_pairs={{0,8},{4,12},{8,0},{12,4},{16,24},{20,28},{24,16},{28,20},{1,9},{5... | collective-permute-start | bytes 393224 | tf_op jit(solution)/shard_map/ppermute | solution.py:299
  81.3 8.1 %collective-permute-start.26 = (f32[64,512]{1,0:T(8,128)S(1)}, f32[64,512]{1,0:T(8,128)S(1)}, u32[]{:S(2)}, u32[]{:S(2)}) collective-permute-start(f32[64,512]{1,0:T(8,128)S(1)} %add.40), channel_id=1, source_target_pairs={{0,16},{4,20},{8,24},{12,28},{16,0},{20,4},{24,8},{28,12},{1,17},{... | collective-permute-start | bytes 393224 | tf_op jit(solution)/shard_map/ppermute | solution.py:299
  83.0 6.5 %collective-permute-start.28 = (f32[64,512]{1,0:T(8,128)S(1)}, f32[64,512]{1,0:T(8,128)S(1)}, u32[]{:S(2)}, u32[]{:S(2)}) collective-permute-start(f32[64,512]{1,0:T(8,128)S(1)} %add.42), channel_id=1, source_target_pairs={{0,24},{4,28},{8,16},{12,20},{16,8},{20,12},{24,0},{28,4},{1,25},{... | collective-permute-start | bytes 393224 | tf_op jit(solution)/shard_map/ppermute | solution.py:299
  90.8 7.2 %collective-permute-start.32 = (f32[64,512]{1,0:T(8,128)S(1)}, f32[64,512]{1,0:T(8,128)S(1)}, u32[]{:S(2)}, u32[]{:S(2)}) collective-permute-start(f32[64,512]{1,0:T(8,128)S(1)} %add_add_fusion.refs_0_.refs_1_), channel_id=1, source_target_pairs={{0,16},{4,20},{8,24},{12,28},{16,0},{20,4},{24,8},{28,12},{1,17},{... | collective-permute-start | bytes 393224 | tf_op jit(solution)/shard_map/ppermute | solution.py:299
  91.8 6.2 %collective-permute-start.34 = (f32[64,512]{1,0:T(8,128)S(1)}, f32[64,512]{1,0:T(8,128)S(1)}, u32[]{:S(2)}, u32[]{:S(2)}) collective-permute-start(f32[64,512]{1,0:T(8,128)S(1)} %add_add_fusion.refs_0_.refs_1_), channel_id=1, source_target_pairs={{0,24},{4,28},{8,16},{12,20},{16,8},{20,12},{24,0},{28,4},{1,25},{... | collective-permute-start | bytes 393224 | tf_op jit(solution)/shard_map/ppermute | solution.py:299
  93.1 6.3 %collective-permute-start.29 = (f32[64,512]{1,0:T(8,128)S(1)}, f32[64,512]{1,0:T(8,128)S(1)}, u32[]{:S(2)}, u32[]{:S(2)}) collective-permute-start(f32[64,512]{1,0:T(8,128)S(1)} %add_add_fusion.refs_0_.refs_1_), channel_id=1, source_target_pairs={{0,4},{4,0},{8,12},{12,8},{16,20},{20,16},{24,28},{28,24},{1,5},{5... | collective-permute-start | bytes 393224 | tf_op jit(solution)/shard_map/ppermute | solution.py:299
  101.2 8.6 %collective-permute-start.45 = (f32[2,64,512]{2,1,0:T(8,128)S(1)}, f32[2,64,512]{2,1,0:T(8,128)S(1)}, u32[]{:S(2)}, u32[]{:S(2)}) collective-permute-start(f32[2,64,512]{2,1,0:T(8,128)S(1)} %get-tuple-element.39), channel_id=1, source_target_pairs={{0,1},{1,0},{2,3},{3,2},{4,5},{5,4},{6,7},{7,6},{8,9},{9,8},{10,11... | collective-permute-start | bytes 786440 | tf_op jit(solution)/shard_map/ppermute | solution.py:296
  109.9 14.3 %collective-permute-start.46 = (f32[2,64,512]{2,1,0:T(8,128)S(1)}, f32[2,64,512]{2,1,0:T(8,128)S(1)}, u32[]{:S(2)}, u32[]{:S(2)}) collective-permute-start(f32[2,64,512]{2,1,0:T(8,128)S(1)} %rev.3), channel_id=1, source_target_pairs={{0,2},{1,3},{2,0},{3,1},{4,6},{5,7},{6,4},{7,5},{8,10},{9,11},{10,... | collective-permute-start | bytes 786440 | tf_op jit(solution)/shard_map/ppermute | solution.py:296
  112.3 12.0 %collective-permute-start.36 = (f32[32,640]{1,0:T(8,128)S(1)}, f32[32,640]{1,0:T(8,128)S(1)}, u32[]{:S(2)}, u32[]{:S(2)}) collective-permute-start(f32[32,640]{1,0:T(8,128)S(1)} %shard_map.92), channel_id=1, source_target_pairs={{0,1},{1,0},{2,3},{3,2},{4,5},{5,4},{6,7},{7,6},{8,9},{9,8},{10,11... | collective-permute-start | bytes 245768 | tf_op jit(solution)/shard_map/ppermute | solution.py:296
  124.2 32.9 %collective-permute-start.47 = (f32[2,64,512]{2,1,0:T(8,128)S(1)}, f32[2,64,512]{2,1,0:T(8,128)S(1)}, u32[]{:S(2)}, u32[]{:S(2)}) collective-permute-start(f32[2,64,512]{2,1,0:T(8,128)S(1)} %add.47.refs_2_), channel_id=1, source_target_pairs={{0,1},{1,0},{2,3},{3,2},{4,5},{5,4},{6,7},{7,6},{8,9},{9,8},{10,11... | collective-permute-start | bytes 786440 | tf_op jit(solution)/shard_map/ppermute | solution.py:296
  124.3 7.7 %collective-permute-start.37 = (f32[32,640]{1,0:T(8,128)S(1)}, f32[32,640]{1,0:T(8,128)S(1)}, u32[]{:S(2)}, u32[]{:S(2)}) collective-permute-start(f32[32,640]{1,0:T(8,128)S(1)} %add.44), channel_id=1, source_target_pairs={{0,2},{1,3},{2,0},{3,1},{4,6},{5,7},{6,4},{7,5},{8,10},{9,11},{10,... | collective-permute-start | bytes 245768 | tf_op jit(solution)/shard_map/ppermute | solution.py:296
  (20 other events, 108.6 us)
